TPU v7x, 32 devices: a whole 2x2x4 slice. The times are simulated.
32 devices in a mesh: groups: 2 (over x), fsdp: 2 (over core), rows: 8 (over z, y).
Axes of the slice: x: 2, y: 2, z: 4, core: 2. Of those that a mesh axis runs over, the one named last changes fastest.
Arguments:
- tokens: bfloat16 [4, 128, 16, 1024], P(('groups', 'fsdp'), 'rows'), parts along dimension 0, may hold values from -6 to 6
- cell_mask: int32 [4, 128, 16], P(('groups', 'fsdp'), 'rows'), parts along dimension 0, may hold values 0 or 1
- shifts: int32 [2], replicated, may hold values from 1 to 15
- projection_in: bfloat16 [1024, 1536], P(('fsdp', 'rows')), may hold values from -2 to 2
- projection_out: bfloat16 [512, 1024], P(('fsdp', 'rows')), may hold values from -0.25 to 0.25
- cotangent: bfloat16 [4, 128, 16, 1024], P(('groups', 'fsdp'), 'rows'), parts along dimension 0, may hold values from -6 to 6
Outputs:
- output: bfloat16 [4, 128, 16, 1024], P(('groups', 'fsdp'), 'rows'), parts along dimension 0
- grad_tokens: bfloat16 [4, 128, 16, 1024], P(('groups', 'fsdp'), 'rows'), parts along dimension 0
- projection_in_grad: float32 [2048, 1536], P(('groups', 'fsdp', 'rows')), parts along dimension 0
- projection_out_grad: float32 [1024, 1024], P(('groups', 'fsdp', 'rows')), parts along dimension 0
There are 2 independent parts, one for each index of `groups`. A program takes and returns all parts, laid end to end along the dimension named above; an argument that names none is the same for every part. Nothing has to cross between parts.
All inputs are finite; a program needn't handle non-finite values. No bound on the sum of `cell_mask` on one device may be relied on, other than what follows from the above.
Results may differ from a plain program's by a relative error of at most 0.011.
Values may be sent and summed in bfloat16 or wider, within the bound.
No kernel may reach another device: no remote copies, remote signals or barrier semaphores. Data moves between devices by JAX's collectives and lax.ppermute only.
A program may use at most 64 MiB of HBM per device.

v0:
```python
import jax
import jax.numpy as jnp
from jax import lax
from jax.sharding import PartitionSpec as P

HEADS = 8
HD = 64
WIN = 16


def shifted(block, axis, distance):
    devices = range(lax.axis_size(axis))
    route = [((i - distance) % len(devices), i) for i in devices]
    return lax.ppermute(block, axis, route)


def roll_columns(grid_field, offset):
    col_count = grid_field.shape[1]
    doubled = jnp.concatenate([grid_field, grid_field], axis=1)
    return lax.dynamic_slice_in_dim(doubled, offset, col_count, 1)


def into_windows(grid_field):
    row_count, col_count, channels = grid_field.shape
    blocks = grid_field.reshape(row_count // WIN, WIN, col_count // WIN, WIN, channels)
    return blocks.transpose(0, 2, 1, 3, 4).reshape(-1, WIN * WIN, channels)


def from_windows(windowed, row_count, col_count):
    channels = windowed.shape[-1]
    blocks = windowed.reshape(row_count // WIN, col_count // WIN, WIN, WIN, channels)
    return blocks.transpose(0, 2, 1, 3, 4).reshape(row_count, col_count, channels)


def normalize(values_f32):
    mean_value = jnp.mean(values_f32, axis=-1, keepdims=True)
    centered = values_f32 - mean_value
    variance = jnp.mean(centered * centered, axis=-1, keepdims=True)
    inv_std = lax.rsqrt(variance + 1e-05)
    return (centered * inv_std, inv_std)


def body(tokens, cell_mask, shifts, projection_in, projection_out, cotangent):
    row_count = tokens.shape[1]
    col_count = tokens.shape[2]
    model_dim = tokens.shape[3]
    hidden_width = HEADS * HD
    score_scale = HD ** (-0.5)
    grid_rows = row_count * lax.axis_size("rows")
    shift_row = shifts[0]
    shift_col = shifts[1]
    full_in, full_out = (
        lax.all_gather(projection_in, ("fsdp", "rows"), axis=0, tiled=True),
        lax.all_gather(projection_out, ("fsdp", "rows"), axis=0, tiled=True),
    )
    mask_wire = cell_mask.astype(jnp.bfloat16)
    next_tokens, next_mask = shifted((tokens, mask_wire), "rows", -1)

    def to_slab(own_rows, next_rows):
        joined = jnp.concatenate([own_rows[0], next_rows[0]], axis=0)
        return roll_columns(lax.dynamic_slice_in_dim(joined, shift_row, row_count, 0), shift_col)

    def to_owner(slab_rows, prev_rows):
        joined = jnp.concatenate([prev_rows, slab_rows], axis=0)
        return lax.dynamic_slice_in_dim(joined, row_count - shift_row, row_count, 0)

    slab_tokens = to_slab(tokens, next_tokens)
    slab_mask = to_slab(mask_wire, next_mask)
    row_ids = (
        lax.axis_index("rows") * row_count + shift_row + jnp.arange(row_count, dtype=jnp.int32)
    ) % grid_rows
    col_ids = (jnp.arange(col_count, dtype=jnp.int32) + shift_col) % col_count
    region = (row_ids < shift_row).astype(jnp.int32)[:, None] * 2 + (col_ids < shift_col).astype(
        jnp.int32
    )[None, :]
    region_win = into_windows(region[:, :, None])[:, :, 0]
    mask_win = into_windows(slab_mask[:, :, None])[:, :, 0] > 0
    token_win = into_windows(slab_tokens)
    window_count = token_win.shape[0]
    window_len = token_win.shape[1]
    allowed = (region_win[:, :, None] == region_win[:, None, :]) & (
        mask_win[:, None, :] | jnp.eye(window_len, dtype=bool)[None]
    )
    normed, inv_std = normalize(token_win.astype(jnp.float32))
    normed_bf = normed.astype(jnp.bfloat16)
    flat_normed = normed_bf.reshape(-1, model_dim)
    packed_heads = jnp.dot(flat_normed, full_in, preferred_element_type=jnp.float32).astype(
        jnp.bfloat16
    )
    packed_heads = packed_heads.reshape(window_count, window_len, 3, HEADS, HD)
    query_heads = packed_heads[:, :, 0]
    key_heads = packed_heads[:, :, 1]
    value_heads = packed_heads[:, :, 2]
    scores = (
        jnp.einsum("wqhd,wkhd->whqk", query_heads, key_heads, preferred_element_type=jnp.float32)
        * score_scale
    )
    scores = jnp.where(allowed[:, None], scores, -1e30)
    row_peak = jnp.max(scores, axis=-1, keepdims=True)
    exp_terms = jnp.exp(scores - row_peak)
    attention = exp_terms / jnp.sum(exp_terms, axis=-1, keepdims=True)
    attention_bf = attention.astype(jnp.bfloat16)
    context = jnp.einsum(
        "whqk,wkhd->wqhd", attention_bf, value_heads, preferred_element_type=jnp.float32
    ).astype(jnp.bfloat16)
    context = context.reshape(window_count, window_len, hidden_width)
    slab_context = roll_columns(from_windows(context, row_count, col_count), col_count - shift_col)
    prev_context = shifted(slab_context, "rows", 1)
    own_context = to_owner(slab_context, prev_context)
    projected = jnp.dot(
        own_context.reshape(-1, hidden_width), full_out, preferred_element_type=jnp.float32
    )
    output = (
        tokens[0].astype(jnp.float32) + projected.reshape(row_count, col_count, model_dim)
    ).astype(jnp.bfloat16)
    next_cotangent = shifted(cotangent, "rows", -1)
    cot_win = into_windows(to_slab(cotangent, next_cotangent))
    flat_cot = cot_win.reshape(-1, model_dim)
    flat_context = context.reshape(-1, hidden_width)
    grad_context = lax.dot_general(
        flat_cot, full_out, (((1,), (1,)), ((), ())), preferred_element_type=jnp.float32
    ).astype(jnp.bfloat16)
    term_out = lax.dot_general(
        flat_context, flat_cot, (((0,), (0,)), ((), ())), preferred_element_type=jnp.float32
    )
    grad_heads = grad_context.reshape(window_count, window_len, HEADS, HD)
    grad_attention = jnp.einsum(
        "wqhd,wkhd->whqk", grad_heads, value_heads, preferred_element_type=jnp.float32
    )
    grad_scores = (
        attention
        * (grad_attention - jnp.sum(grad_attention * attention, axis=-1, keepdims=True))
        * score_scale
    ).astype(jnp.bfloat16)
    grad_query = jnp.einsum(
        "whqk,wkhd->wqhd", grad_scores, key_heads, preferred_element_type=jnp.float32
    )
    grad_key = jnp.einsum(
        "whqk,wqhd->wkhd", grad_scores, query_heads, preferred_element_type=jnp.float32
    )
    grad_value = jnp.einsum(
        "whqk,wqhd->wkhd", attention_bf, grad_heads, preferred_element_type=jnp.float32
    )
    grad_packed = (
        jnp.stack([grad_query, grad_key, grad_value], axis=2)
        .astype(jnp.bfloat16)
        .reshape(-1, 3 * hidden_width)
    )
    term_in = lax.dot_general(
        flat_normed, grad_packed, (((0,), (0,)), ((), ())), preferred_element_type=jnp.float32
    )
    grad_normed = lax.dot_general(
        grad_packed, full_in, (((1,), (1,)), ((), ())), preferred_element_type=jnp.float32
    )
    grad_normed = grad_normed.reshape(window_count, window_len, model_dim)
    grad_win = (
        cot_win.astype(jnp.float32)
        + inv_std
        * (
            grad_normed
            - jnp.mean(grad_normed, axis=-1, keepdims=True)
            - normed * jnp.mean(grad_normed * normed, axis=-1, keepdims=True)
        )
    ).astype(jnp.bfloat16)
    slab_grad = roll_columns(from_windows(grad_win, row_count, col_count), col_count - shift_col)
    prev_grad = shifted(slab_grad, "rows", 1)
    own_grad = to_owner(slab_grad, prev_grad)
    grad_in, grad_out = (
        lax.psum_scatter(term_in, ("fsdp", "rows"), scatter_dimension=0, tiled=True),
        lax.psum_scatter(term_out, ("fsdp", "rows"), scatter_dimension=0, tiled=True),
    )
    return (output[None], own_grad[None], grad_in, grad_out)


def solution(mesh):
    placed = (
        P(("groups", "fsdp"), "rows", None, None),
        P(("groups", "fsdp"), "rows", None),
        P(),
        P(("fsdp", "rows"), None),
        P(("fsdp", "rows"), None),
        P(("groups", "fsdp"), "rows", None, None),
    )
    return jax.shard_map(
        body,
        mesh=mesh,
        in_specs=placed,
        out_specs=(
            P(("groups", "fsdp"), "rows", None, None),
            P(("groups", "fsdp"), "rows", None, None),
            P(("groups", "fsdp", "rows"), None),
            P(("groups", "fsdp", "rows"), None),
        ),
        check_vma=False,
    )
```

profile of v0, /device:TPU:0, one launch (start us, length us, event | category | flops | bytes accessed | tf_op | source)
XLA Modules:
  0.0 278.8 jit_solution(13945911961746731159)
XLA Ops:
  7.2 0.7 all-gather.3.cloned.1.call-update
  8.0 0.7 convert_element_type.146
  8.7 6.0 %collective-permute-start.1 = (bf16[1,16,16]{2,1,0:T(8,128)(2,1)S(1)}, bf16[1,16,16]{2,1,0:T(8,128)(2,1)S(1)}, u32[]{:S(2)}, u32[]{:S(2)}) collective-permute-start(bf16[1,16,16]{2,1,0:T(8,128)(2,1)S(1)} %convert_element_type.146), channel_id=1, source_target_pairs={{1,0},{2,1},{3,2},{4,3},{5,4},{6,5},{7,6},{0,7},{9,8},{10,9},{11,1... | collective-permute-start | bytes 1544 | tf_op jit(solution)/shard_map/ppermute | solution.py:14
  14.7 0.5 collective-permute-start.3
  15.2 1.4 collective-permute-start
  16.7 0.7 convert_bitcast_fusion
  17.4 1.3 fusion.66
  18.7 0.7 compare_convert_fusion
  19.9 0.6 compare_select_fusion.4
  24.9 19.1 %collective-permute-done = bf16[1,16,16,1024]{3,2,1,0:T(8,128)(2,1)S(1)} collective-permute-done((bf16[1,16,16,1024]{3,2,1,0:T(8,128)(2,1)}, bf16[1,16,16,1024]{3,2,1,0:T(8,128)(2,1)S(1)}, u32[]{:S(2)}, u32[]{:S(2)}) %collective-permute-start) | collective-permute-done | bytes 524320 | tf_op jit(solution)/shard_map/ppermute | solution.py:14
  44.0 1.2 fusion.39
  47.0 22.1 %all-gather.3.cloned.1.call-done = bf16[1024,1536]{1,0:T(8,128)(2,1)} async-done(((bf16[64,1536]{1,0:T(8,128)(2,1)}), bf16[1024,1536]{1,0:T(8,128)(2,1)}) %all-gather.3.cloned.1.call-update) | async-done | bytes 3145744 | tf_op jit(solution)/shard_map/all_gather | solution.py:53
  69.1 3.8 %convolution_convert_fusion = bf16[256,1536]{1,0:T(8,128)(2,1)} fusion(bf16[256,1024]{1,0:T(8,128)(2,1)S(1)} %fusion.29, bf16[1024,1536]{1,0:T(8,128)(2,1)} %all-gather.3.cloned.1.call-done), kind=kOutput, calls=%fused_computation.2 | convolution fusion | flops 805699584 | bytes 4456448 | tf_op jit(solution)/shard_map/dot_general | solution.py:87
  72.9 1.4 copy.21
  74.3 2.2 fusion.67
  76.5 1.9 convolution_convert_fusion.2
  78.4 0.7 copy-done.2
  79.1 1.8 fusion.68
  80.9 27.2 %all-gather.5.cloned.1.call-done = bf16[512,1024]{1,0:T(8,128)(2,1)} async-done(((bf16[32,1024]{1,0:T(8,128)(2,1)}), bf16[512,1024]{1,0:T(8,128)(2,1)}) %all-gather.5.cloned.1.call-update) | async-done | bytes 1048592 | tf_op jit(solution)/shard_map/all_gather | solution.py:54
  108.1 1.7 convolution_convert_fusion.1
  110.0 1.8 fusion.49
  111.7 4.2 %fusion.14 = bf16[1,256,1,8,64]{1,4,3,2,0:T(8,128)(2,1)S(1)} fusion(f32[8,256,256]{1,2,0:T(8,128)} %fusion.49, bf16[1,256,3,8,64]{1,4,3,2,0:T(8,128)(2,1)S(1)} %bitcast.119, f32[8,256,256]{1,2,0:T(8,128)} %get-tuple-element.11, f32[8,256]{1,0:T(8,128)S(1)} %get-tuple-element.10), kind=kOutput, calls=%fused_computation.15 | convolution fusion | flops 70781184 | bytes 8929280 | tf_op jit(solution)/shard_map/whqk,wkhd->wqhd/dot_general | solution.py:135
  116.0 5.1 %fusion.17 = bf16[1,256,1,8,64]{1,4,3,2,0:T(8,128)(2,1)} fusion(f32[8,256,256]{1,2,0:T(8,128)} %fusion.49, bf16[1,256,3,8,64]{1,4,3,2,0:T(8,128)(2,1)S(1)} %bitcast.120, f32[8,256,256]{1,2,0:T(8,128)} %get-tuple-element.11, f32[8,256]{1,0:T(8,128)S(1)} %get-tuple-element.10), kind=kOutput, calls=%fused_computation.16 | convolution fusion | flops 70781184 | bytes 8929280 | tf_op jit(solution)/shard_map/whqk,wqhd->wkhd/dot_general | solution.py:138
  121.1 2.2 convolution_bitcast_fusion
  123.3 3.8 %fusion.31 = f32[1024,1536]{1,0:T(8,128)} fusion(bf16[256,1536]{0,1:T(8,128)(2,1)S(1)} %bitcast.112, f32[1,256,1,1,1,1,1024]{6,1,5,4,3,2,0:T(8,128)S(1)} %bitcast.109, f32[256]{0:T(256)S(1)} %add_rsqrt_fusion, f32[256]{0:T(256)S(1)} %div.24), kind=kOutput, calls=%fused_computation.50 | convolution fusion | flops 806092800 | bytes 8128512 | tf_op jit(solution)/shard_map/dot_general | solution.py:149
  129.2 3.1 %fusion.64 = (f32[256]{0:T(256)S(1)}, f32[256]{0:T(256)S(1)}, f32[256,1024]{1,0:T(8,128)S(1)}) fusion(f32[256]{0:T(256)S(1)} %add_rsqrt_fusion, f32[256]{0:T(256)S(1)} %div.24, bf16[16,16,1024]{2,1,0:T(8,128)(2,1)S(1)} %get-tuple-element.7, bf16[256,1536]{0,1:T(8,128)(2,1)S(1)} %bitcast.113, bf16[1024,1536]{1,0:T(8,128)(2,1)} %all-gather.3.cloned.1.call-done), kind=kOutput, calls=%fused_computation.106 | convolution fusion | flops 806878720 | bytes 5509120 | tf_op jit(solution)/shard_map/dot_general | solution.py:152
  133.9 1.5 collective-permute-start.2
  136.7 27.6 %collective-permute-done.2 = bf16[16,16,512]{2,1,0:T(8,128)(2,1)S(1)} collective-permute-done((bf16[16,16,512]{2,1,0:T(8,128)(2,1)S(1)}, bf16[16,16,512]{2,1,0:T(8,128)(2,1)S(1)}, u32[]{:S(2)}, u32[]{:S(2)}) %collective-permute-start.2) | collective-permute-done | bytes 262176 | tf_op jit(solution)/shard_map/ppermute | solution.py:14
  164.2 1.3 fusion.13
  165.5 1.0 fusion.34
  166.5 16.6 %reduce-scatter.5.cloned.1.call-done = f32[32,1024]{1,0:T(8,128)} async-done(((f32[512,1024]{1,0:T(8,128)}), f32[32,1024]{1,0:T(8,128)}) %reduce-scatter.5.cloned.1.call-update) | async-done | bytes 131088 | tf_op jit(solution)/shard_map/reduce_scatter | solution.py:170
  183.2 89.1 %reduce-scatter.3.cloned.1.call-done = f32[64,1536]{1,0:T(8,128)} async-done(((f32[1024,1536]{1,0:T(8,128)}), f32[64,1536]{1,0:T(8,128)}) %reduce-scatter.3.cloned.1.call-update) | async-done | bytes 393232 | tf_op jit(solution)/shard_map/reduce_scatter | solution.py:169
  (45 shorter events, 4.9 us)
Async XLA Ops:
  7.2 38.5 %copy-start.4 = (bf16[1,16,16,1024]{3,2,1,0:T(8,128)(2,1)S(1)}, bf16[1,16,16,1024]{3,2,1,0:T(8,128)(2,1)}, u32[]{:S(2)}) copy-start(bf16[1,16,16,1024]{3,2,1,0:T(8,128)(2,1)} %param.11) | copy-start | bytes 1572868
  7.2 61.9 %all-gather.3.cloned.1.call-start = ((), (), s32[]{:S(2)}) async-start(), calls=%async_computation.2 | async-start | bytes 3342336 | tf_op jit(solution)/shard_map/all_gather | solution.py:53
  7.9 100.2 %all-gather.5.cloned.1.call-start = ((), (), s32[]{:S(2)}) async-start(), calls=%async_computation.3 | async-start | bytes 1114112 | tf_op jit(solution)/shard_map/all_gather | solution.py:54
  8.7 15.8 %collective-permute-start.1 = (bf16[1,16,16]{2,1,0:T(8,128)(2,1)S(1)}, bf16[1,16,16]{2,1,0:T(8,128)(2,1)S(1)}, u32[]{:S(2)}, u32[]{:S(2)}) collective-permute-start(bf16[1,16,16]{2,1,0:T(8,128)(2,1)S(1)} %convert_element_type.146), channel_id=1, source_target_pairs={{1,0},{2,1},{3,2},{4,3},{5,4},{6,5},{7,6},{0,7},{9,8},{10,9},{11,1... | collective-permute-start | bytes 1544 | tf_op jit(solution)/shard_map/ppermute | solution.py:14
  14.7 31.0 %collective-permute-start.3 = (bf16[1,16,16,1024]{3,2,1,0:T(8,128)(2,1)}, bf16[1,16,16,1024]{3,2,1,0:T(8,128)(2,1)S(1)}, u32[]{:S(2)}, u32[]{:S(2)}) collective-permute-start(bf16[1,16,16,1024]{3,2,1,0:T(8,128)(2,1)} %param.11), channel_id=1, source_target_pairs={{1,0},{2,1},{3,2},{4,3},{5,4},{6,5},{7,6},{0,7},{9,8},{10,9},{11,1... | collective-permute-start | bytes 1572872 | tf_op jit(solution)/shard_map/ppermute | solution.py:14
  15.2 28.8 %collective-permute-start = (bf16[1,16,16,1024]{3,2,1,0:T(8,128)(2,1)}, bf16[1,16,16,1024]{3,2,1,0:T(8,128)(2,1)S(1)}, u32[]{:S(2)}, u32[]{:S(2)}) collective-permute-start(bf16[1,16,16,1024]{3,2,1,0:T(8,128)(2,1)} %param.6), channel_id=1, source_target_pairs={{1,0},{2,1},{3,2},{4,3},{5,4},{6,5},{7,6},{0,7},{9,8},{10,9},{11,1... | collective-permute-start | bytes 1572872 | tf_op jit(solution)/shard_map/ppermute | solution.py:14
  16.6 166.6 %reduce-scatter.5.cloned.1.call-start = ((), (), s32[]{:S(2)}) async-start(), calls=%async_computation.5 | async-start | bytes 2228224 | tf_op jit(solution)/shard_map/reduce_scatter | solution.py:170
  78.4 0.7 copy-start.2
  80.9 191.4 %reduce-scatter.3.cloned.1.call-start = ((), (), s32[]{:S(2)}) async-start(), calls=%async_computation.4 | async-start | bytes 6684672 | tf_op jit(solution)/shard_map/reduce_scatter | solution.py:169
  121.1 2.2 copy-start.5
  127.2 1.4 copy-start.3
  132.4 31.8 %copy-start = (bf16[512,1024]{1,0:T(8,128)(2,1)S(1)}, bf16[512,1024]{1,0:T(8,128)(2,1)}, u32[]{:S(2)}) copy-start(bf16[512,1024]{1,0:T(8,128)(2,1)} %all-gather.5.cloned.1.call-done) | copy-start | bytes 3145732
  132.4 31.8 %copy-start.1 = (bf16[1,16,16,1024]{3,2,1,0:T(8,128)(2,1)S(1)}, bf16[1,16,16,1024]{3,2,1,0:T(8,128)(2,1)}, u32[]{:S(2)}) copy-start(bf16[1,16,16,1024]{3,2,1,0:T(8,128)(2,1)} %param.6) | copy-start | bytes 1572868
  133.2 32.3 %collective-permute-start.4 = (bf16[16,16,1024]{2,1,0:T(8,128)(2,1)S(1)}, bf16[16,16,1024]{2,1,0:T(8,128)(2,1)S(1)}, u32[]{:S(2)}, u32[]{:S(2)}) collective-permute-start(bf16[16,16,1024]{2,1,0:T(8,128)(2,1)S(1)} %fusion.35), channel_id=1, source_target_pairs={{7,0},{0,1},{1,2},{2,3},{3,4},{4,5},{5,6},{6,7},{15,8},{8,9},{9,10... | collective-permute-start | bytes 1572872 | tf_op jit(solution)/shard_map/ppermute | solution.py:14
  133.9 30.3 %collective-permute-start.2 = (bf16[16,16,512]{2,1,0:T(8,128)(2,1)S(1)}, bf16[16,16,512]{2,1,0:T(8,128)(2,1)S(1)}, u32[]{:S(2)}, u32[]{:S(2)}) collective-permute-start(bf16[16,16,512]{2,1,0:T(8,128)(2,1)S(1)} %fusion.46), channel_id=1, source_target_pairs={{7,0},{0,1},{1,2},{2,3},{3,4},{4,5},{5,6},{6,7},{15,8},{8,9},{9,10... | collective-permute-start | bytes 786440 | tf_op jit(solution)/shard_map/ppermute | solution.py:14
Sparse Core Ops, SparseCore 0:
  10.2 58.8 all-gather.2
  71.3 36.7 all-gather.4
  112.4 70.6 reduce-scatter.4
  188.0 84.2 reduce-scatter.2
where the time goes:
time: 279 us
  waiting for transfers between devices  202 us (72%)
  matrix products  32.9 us (12%)
  between operations  20.9 us (7%)
  starting transfers between devices  10.1 us (4%)
  other arithmetic  8.02 us (3%)
  local copies, waits for them, and re-layouts  4.47 us (2%)
    reduce_scatter x1, waiting for transfers between devices, body(): lax.psum_scatter(term_in, ('fsdp', 'rows'), scatter_dimension=0, tiled=True)  89.1 us
    ppermute x5, waiting for transfers between devices, shifted(): return lax.ppermute(block, axis, route)  46.7 us
    all_gather x1, waiting for transfers between devices, body(): lax.all_gather(projection_out, ('fsdp', 'rows'), axis=0, tiled=True)  27.2 us
    all_gather x1, waiting for transfers between devices, body(): lax.all_gather(projection_in, ('fsdp', 'rows'), axis=0, tiled=True)  22.1 us
    reduce_scatter x1, waiting for transfers between devices, body(): lax.psum_scatter(term_out, ('fsdp', 'rows'), scatter_dimension=0, tiled=T...  16.6 us
    ppermute x5, starting transfers between devices, shifted(): return lax.ppermute(block, axis, route)  9.92 us
  transfers between devices with their start and end apart: 9, of which 6 were waited for; matrix products, arithmetic and copies ran while one was open for 16% of the time, Pallas kernels for 0%

commit v1 on v0

v1 whole, which is shorter than its diff:
```python
import jax
import jax.numpy as jnp
import numpy as np
from jax import lax
from jax.sharding import PartitionSpec as P

HEADS = 8
HD = 64
WIN = 16


def stage_masks(rows):
    bits = [1 << b for b in range(rows.bit_length() - 1)]
    far = bits[:1:-1]
    return (far + bits[:2], far + bits[:2][::-1])


def slot_masks(rows, core):
    masks = [0]
    for m in stage_masks(rows)[core]:
        masks = masks + [a ^ m for a in masks]
    return np.array(masks, np.int32)


def exchange(block, rows, stage):
    masks = stage_masks(rows)
    pairs = [
        (c * rows + i, c * rows + (i ^ masks[c][stage])) for c in range(2) for i in range(rows)
    ]
    return lax.ppermute(block, ("fsdp", "rows"), pairs)


def swap_cores(block):
    return lax.ppermute(block, "fsdp", [(0, 1), (1, 0)])


def shifted(block, rows, distance):
    return lax.ppermute(block, "rows", [((i - distance) % rows, i) for i in range(rows)])


def slot_tables(rows):
    core = lax.axis_index("fsdp")
    me = lax.axis_index("rows")
    m0 = jnp.asarray(slot_masks(rows, 0))
    m1 = jnp.asarray(slot_masks(rows, 1))
    own = jnp.where(core == 0, m0, m1) ^ me
    other = jnp.where(core == 0, m1, m0) ^ me
    return core, own, other


def gather_rows(shard, rows, core, own, other):
    stages = len(stage_masks(rows)[0])
    held = shard[None]
    for stage in range(stages):
        held = jnp.concatenate([held, exchange(held, rows, stage)], axis=0)
    theirs = swap_cores(held)
    both = jnp.concatenate([held, theirs], axis=0)
    where = jnp.concatenate([core * rows + own, (1 - core) * rows + other])
    slot_of = jnp.argsort(where)
    return jnp.take(both, slot_of, axis=0).reshape(-1, shard.shape[-1])


def scatter_rows(term, rows, core, own, other):
    stages = len(stage_masks(rows)[0])
    blocks = term.reshape(2 * rows, -1, term.shape[-1])
    keep = jnp.take(blocks, core * rows + own, axis=0)
    send = jnp.take(blocks, (1 - core) * rows + other, axis=0).astype(jnp.bfloat16)
    keep = keep + swap_cores(send).astype(jnp.float32)
    for stage in range(stages - 1, -1, -1):
        half = keep.shape[0] // 2
        arrived = exchange(keep[half:].astype(jnp.bfloat16), rows, stage)
        keep = keep[:half] + arrived.astype(jnp.float32)
    return keep[0]


def body(tokens, cell_mask, shifts, projection_in, projection_out, cotangent):
    rows = lax.axis_size("rows")
    row_count, col_count, model_dim = tokens.shape[1:]
    cells = row_count * col_count
    hidden = HEADS * HD
    scale = HD ** (-0.5)
    s_row, s_col = shifts[0], shifts[1]
    core, own, other = slot_tables(rows)
    own_tokens = tokens.reshape(cells, model_dim)
    own_cot = cotangent.reshape(cells, model_dim)
    next_tokens = shifted(own_tokens, rows, -1)
    own_mask = cell_mask.astype(jnp.bfloat16).reshape(cells, 1)
    next_mask = shifted(own_mask, rows, -1)
    next_cot = shifted(own_cot, rows, -1)
    full_in = gather_rows(projection_in, rows, core, own, other)
    full_out = gather_rows(projection_out, rows, core, own, other)
    cell = jnp.arange(cells, dtype=jnp.int32)
    cell_row, cell_col = cell // col_count, cell % col_count
    borrowed = cell_row < s_row
    x = jnp.where(borrowed[:, None], next_tokens, own_tokens)
    cot = jnp.where(borrowed[:, None], next_cot, own_cot)
    key_ok = jnp.where(borrowed, next_mask[:, 0], own_mask[:, 0]) > 0
    last = lax.axis_index("rows") == rows - 1
    region = 2 * (borrowed & last).astype(jnp.int32) + (cell_col < s_col).astype(jnp.int32)
    allowed = (region[:, None] == region[None, :]) & (
        key_ok[None, :] | (cell[:, None] == cell[None, :])
    )
    xf = x.astype(jnp.float32)
    mean = jnp.mean(xf, axis=-1, keepdims=True)
    centered = xf - mean
    inv_std = lax.rsqrt(jnp.mean(centered * centered, axis=-1, keepdims=True) + 1e-05)
    normed = centered * inv_std
    normed_bf = normed.astype(jnp.bfloat16)
    packed = jnp.dot(normed_bf, full_in, preferred_element_type=jnp.float32).astype(jnp.bfloat16)
    packed = packed.reshape(cells, 3, HEADS, HD)
    q, k, v = packed[:, 0], packed[:, 1], packed[:, 2]
    f32 = jnp.float32
    scores = jnp.einsum("qhd,khd->hqk", q, k, preferred_element_type=f32) * scale
    scores = jnp.where(allowed[None], scores, -1e30)
    exp_terms = jnp.exp(scores - jnp.max(scores, axis=-1, keepdims=True))
    attention = exp_terms / jnp.sum(exp_terms, axis=-1, keepdims=True)
    attention_bf = attention.astype(jnp.bfloat16)
    context = jnp.einsum("hqk,khd->qhd", attention_bf, v, preferred_element_type=f32)
    context = context.astype(jnp.bfloat16).reshape(cells, hidden)
    own_context = jnp.where(borrowed[:, None], shifted(context, rows, 1), context)
    output = (
        own_tokens.astype(f32) + jnp.dot(own_context, full_out, preferred_element_type=f32)
    ).astype(jnp.bfloat16)
    grad_context = lax.dot_general(
        cot, full_out, (((1,), (1,)), ((), ())), preferred_element_type=f32
    ).astype(jnp.bfloat16)
    term_out = lax.dot_general(context, cot, (((0,), (0,)), ((), ())), preferred_element_type=f32)
    grad_out = scatter_rows(term_out, rows, core, own, other)
    gh = grad_context.reshape(cells, HEADS, HD)
    grad_attention = jnp.einsum("qhd,khd->hqk", gh, v, preferred_element_type=f32)
    grad_scores = (
        attention
        * (grad_attention - jnp.sum(grad_attention * attention, axis=-1, keepdims=True))
        * scale
    ).astype(jnp.bfloat16)
    gq = jnp.einsum("hqk,khd->qhd", grad_scores, k, preferred_element_type=f32)
    gk = jnp.einsum("hqk,qhd->khd", grad_scores, q, preferred_element_type=f32)
    gv = jnp.einsum("hqk,qhd->khd", attention_bf, gh, preferred_element_type=f32)
    gp = jnp.stack([gq, gk, gv], axis=1).astype(jnp.bfloat16).reshape(cells, 3 * hidden)
    term_in = lax.dot_general(normed_bf, gp, (((0,), (0,)), ((), ())), preferred_element_type=f32)
    grad_in = scatter_rows(term_in, rows, core, own, other)
    gn = lax.dot_general(gp, full_in, (((1,), (1,)), ((), ())), preferred_element_type=f32)
    grad_win = (
        cot.astype(f32)
        + inv_std
        * (
            gn
            - jnp.mean(gn, axis=-1, keepdims=True)
            - normed * jnp.mean(gn * normed, axis=-1, keepdims=True)
        )
    ).astype(jnp.bfloat16)
    own_grad = jnp.where(borrowed[:, None], shifted(grad_win, rows, 1), grad_win)
    shape = tokens.shape
    return (output.reshape(shape), own_grad.reshape(shape), grad_in, grad_out)


def solution(mesh):
    placed = (
        P(("groups", "fsdp"), "rows", None, None),
        P(("groups", "fsdp"), "rows", None),
        P(),
        P(("fsdp", "rows"), None),
        P(("fsdp", "rows"), None),
        P(("groups", "fsdp"), "rows", None, None),
    )
    return jax.shard_map(
        body,
        mesh=mesh,
        in_specs=placed,
        out_specs=(
            P(("groups", "fsdp"), "rows", None, None),
            P(("groups", "fsdp"), "rows", None, None),
            P(("groups", "fsdp", "rows"), None),
            P(("groups", "fsdp", "rows"), None),
        ),
        check_vma=False,
    )
```

time: 279 us -> 171 us (0.61)
  waiting for transfers between devices: 202 us -> 44.4 us
  starting transfers between devices: 10.1 us -> 49.8 us
  local copies, waits for them, and re-layouts: 4.47 us -> 31.9 us
  between operations: 20.9 us -> 1.15 us
  other arithmetic: 8.02 us -> 22.5 us
  matrix products: 32.9 us -> 20.8 us
    reduce_scatter x2 -> x0, waiting for transfers between devices: 106 us -> none  [the longest x1 89.1 us: body(): lax.psum_scatter(term_in, ('fsdp', 'rows'), scatter_dimension=0, tiled=True)]
    all_gather x2 -> x0, waiting for transfers between devices: 49.3 us -> none  [the longest x1 27.2 us: body(): lax.all_gather(projection_out, ('fsdp', 'rows'), axis=0, tiled=True)]
    ppermute x5 -> x21, starting transfers between devices: 9.92 us -> 49.8 us  [the longest x12 37.7 us: exchange(): return lax.ppermute(block, ('fsdp', 'rows'), pairs)]
    gather x0 -> x6, local copies, waits for them, and re-layouts: none -> 14.5 us  [the longest x2 5.14 us: scatter_rows(): keep = jnp.take(blocks, core * rows + own, axis=0)]
    dot_general x11, matrix products: 30.7 us -> 18.6 us  [the longest x1 4.25 us: body(): gk = jnp.einsum('hqk,qhd->khd', grad_scores, q, preferred_element_type=f32)]
    unnamed x12 -> x42, local copies, waits for them, and re-layouts: 0.74 us -> 11.3 us
    select_n x0 -> x8, other arithmetic: none -> 3.91 us  [the longest x4 2.81 us: gather_rows(): return jnp.take(both, slot_of, axis=0).reshape(-1, shard.shape[-1])]
    add x1 -> x7, other arithmetic: 0.07 us -> 3.98 us  [the longest x2 2.28 us: scatter_rows(): keep = keep + swap_cores(send).astype(jnp.float32)]
  transfers between devices with their start and end apart: 9 -> 21, of which waited for: 6 -> 7; matrix products, arithmetic and copies ran while one was open for 16% -> 22% of each run, Pallas kernels for 0% -> 0%
where the time goes in v1:
time: 171 us
  starting transfers between devices  49.8 us (29%)
  waiting for transfers between devices  44.4 us (26%)
  local copies, waits for them, and re-layouts  31.9 us (19%)
  other arithmetic  22.5 us (13%)
  matrix products  20.8 us (12%)
    ppermute x12, waiting for transfers between devices, exchange(): return lax.ppermute(block, ('fsdp', 'rows'), pairs)  42.4 us
    ppermute x12, starting transfers between devices, exchange(): return lax.ppermute(block, ('fsdp', 'rows'), pairs)  37.7 us
    ppermute x5, starting transfers between devices, shifted(): lax.ppermute(block, 'rows', [((i - distance) % rows, i) for i in range(ro...  11.4 us
    unnamed x42, local copies, waits for them, and re-layouts  11.3 us
    gather x2, local copies, waits for them, and re-layouts, scatter_rows(): keep = jnp.take(blocks, core * rows + own, axis=0)  5.14 us
    gather x2, local copies, waits for them, and re-layouts, scatter_rows(): jnp.take(blocks, (1 - core) * rows + other, axis=0).astype(jnp.bfloat16)  4.87 us
    gather x2, local copies, waits for them, and re-layouts, gather_rows(): return jnp.take(both, slot_of, axis=0).reshape(-1, shard.shape[-1])  4.47 us
    dot_general x1, matrix products, body(): gk = jnp.einsum('hqk,qhd->khd', grad_scores, q, preferred_element_type=f32)  4.25 us
  transfers between devices with their start and end apart: 21, of which 7 were waited for; matrix products, arithmetic and copies ran while one was open for 22% of the time, Pallas kernels for 0%

profile of v1, /device:TPU:0, one launch (start us, length us, event | category | flops | bytes accessed | tf_op | source)
XLA Modules:
  0.0 170.6 jit_solution(5628978295451794212)
XLA Ops:
  1.5 6.0 %collective-permute-start.5 = (bf16[256,1]{0,1:T(2,128)(2,1)S(1)}, bf16[256,1]{0,1:T(2,128)(2,1)S(1)}, u32[]{:S(2)}, u32[]{:S(2)}) collective-permute-start(bf16[256,1]{0,1:T(2,128)(2,1)S(1)} %reshape.247), channel_id=1, source_target_pairs={{1,0},{2,1},{3,2},{4,3},{5,4},{6,5},{7,6},{0,7},{9,8},{10,9},{11,1... | collective-permute-start | bytes 1544 | tf_op jit(solution)/shard_map/ppermute | solution.py:38
  7.5 2.9 %collective-permute-start.1 = (bf16[1,64,1536]{2,1,0:T(8,128)(2,1)}, bf16[1,64,1536]{2,1,0:T(8,128)(2,1)S(1)}, u32[]{:S(2)}, u32[]{:S(2)}) collective-permute-start(bf16[1,64,1536]{2,1,0:T(8,128)(2,1)} %bitcast.94), channel_id=1, source_target_pairs={{0,4},{1,5},{2,6},{3,7},{4,0},{5,1},{6,2},{7,3},{8,12},{9,13},{10,... | collective-permute-start | bytes 589832 | tf_op jit(solution)/shard_map/ppermute | solution.py:30
  14.3 1.5 constant_dynamic-update-slice_fusion.9
  15.8 1.6 constant_dynamic-update-slice_fusion.4
  26.6 10.4 %collective-permute-done.8 = bf16[2,32,1024]{2,1,0:T(8,128)(2,1)S(1)} collective-permute-done((bf16[2,32,1024]{2,1,0:T(8,128)(2,1)S(1)}, bf16[2,32,1024]{2,1,0:T(8,128)(2,1)S(1)}, u32[]{:S(2)}, u32[]{:S(2)}) %collective-permute-start.8) | collective-permute-done | bytes 131104 | tf_op jit(solution)/shard_map/ppermute | solution.py:30
  37.9 7.1 %collective-permute-start.9 = (bf16[4,32,1024]{2,1,0:T(8,128)(2,1)S(1)}, bf16[4,32,1024]{2,1,0:T(8,128)(2,1)S(1)}, u32[]{:S(2)}, u32[]{:S(2)}) collective-permute-start(bf16[4,32,1024]{2,1,0:T(8,128)(2,1)S(1)} %pad_maximum_fusion.5), channel_id=1, source_target_pairs={{0,2},{1,3},{2,0},{3,1},{4,6},{5,7},{6,4},{7,5},{8,9},{9,8},{10,11... | collective-permute-start | bytes 786440 | tf_op jit(solution)/shard_map/ppermute | solution.py:30
  46.4 7.1 %collective-permute-start.3 = (bf16[4,64,1536]{2,1,0:T(8,128)(2,1)S(1)}, bf16[4,64,1536]{2,1,0:T(8,128)(2,1)S(1)}, u32[]{:S(2)}, u32[]{:S(2)}) collective-permute-start(bf16[4,64,1536]{2,1,0:T(8,128)(2,1)S(1)} %pad_maximum_fusion.1), channel_id=1, source_target_pairs={{0,2},{1,3},{2,0},{3,1},{4,6},{5,7},{6,4},{7,5},{8,9},{9,8},{10,11... | collective-permute-start | bytes 2359304 | tf_op jit(solution)/shard_map/ppermute | solution.py:30
  55.7 7.7 %collective-permute-done.3 = bf16[4,64,1536]{2,1,0:T(8,128)(2,1)S(1)} collective-permute-done((bf16[4,64,1536]{2,1,0:T(8,128)(2,1)S(1)}, bf16[4,64,1536]{2,1,0:T(8,128)(2,1)S(1)}, u32[]{:S(2)}, u32[]{:S(2)}) %collective-permute-start.3) | collective-permute-done | bytes 786464 | tf_op jit(solution)/shard_map/ppermute | solution.py:30
  66.6 1.8 %gather_fusion.1 = bf16[16,32,1024]{2,1,0:T(8,128)(2,1)S(1)} fusion(bf16[16,32,1024]{2,1,0:T(8,128)(2,1)} %constant_dynamic-update-slice_fusion.5, s32[1024]{0:T(1024)S(1)} %pad_clamp_fusion.2), kind=kCustom, calls=%fused_computation.5 | custom fusion | bytes 2097216 | tf_op jit(solution)/shard_map/jit(_take)/gather | solution.py:60
  71.4 2.7 %constant_dynamic-update-slice_fusion = bf16[16,64,1536]{2,1,0:T(8,128)(2,1)} fusion(bf16[16,64,1536]{2,1,0:T(8,128)(2,1)} %constant_dynamic-update-slice_fusion.1, bf16[8,64,1536]{2,1,0:T(8,128)(2,1)} %collective-permute-done.4), kind=kLoop, calls=%fused_computation.91 | loop fusion | bytes 3145728 | tf_op jit(solution)/shard_map/concatenate | solution.py:57
  74.0 2.6 %gather_fusion = bf16[16,64,1536]{2,1,0:T(8,128)(2,1)S(1)} fusion(bf16[16,64,1536]{2,1,0:T(8,128)(2,1)} %constant_dynamic-update-slice_fusion, s32[1024]{0:T(1024)S(1)} %pad_clamp_fusion.2), kind=kCustom, calls=%fused_computation.4 | custom fusion | bytes 6291520 | tf_op jit(solution)/shard_map/jit(_take)/gather | solution.py:60
  76.7 2.0 %broadcast_select_fusion = bf16[16,64,1536]{2,1,0:T(8,128)(2,1)} fusion(bf16[16,64,1536]{2,1,0:T(8,128)(2,1)S(1)} %gather_fusion, pred[16]{0:T(512)(128)(4,1)S(1)} %compare_and_fusion.2), kind=kLoop, calls=%fused_computation.11 | loop fusion | flops 1572864 | bytes 6291472 | tf_op jit(solution)/shard_map/jit(_take)/select_n | solution.py:60
  81.1 2.2 %fusion.74 = (f32[8,256]{1,0:T(8,128)S(1)}, f32[8,256,256]{1,2,0:T(8,128)}) fusion(pred[256,256]{0,1:T(8,128)(4,1)S(1)} %fusion.49, bf16[256,3,8,64]{0,3,2,1:T(8,128)(2,1)S(1)} %bitcast.101), kind=kOutput, calls=%fused_computation.142 | convolution fusion | flops 69206272 | bytes 2695168 | tf_op jit(solution)/shard_map/sub | solution.py:115
  85.7 3.0 %fusion.27 = bf16[256,1,8,64]{0,3,2,1:T(8,128)(2,1)S(1)} fusion(f32[8,256,256]{1,2,0:T(8,128)S(1)} %fusion.51, bf16[256,3,8,64]{0,3,2,1:T(8,128)(2,1)S(1)} %bitcast.103, f32[8,256,256]{1,2,0:T(8,128)} %get-tuple-element.23, f32[8,256]{1,0:T(8,128)S(1)} %get-tuple-element.22), kind=kOutput, calls=%fused_computation.39 | convolution fusion | flops 70912256 | bytes 8929280 | tf_op jit(solution)/shard_map/hqk,khd->qhd/dot_general | solution.py:136
  88.6 4.3 %fusion.24 = bf16[256,1,8,64]{0,3,2,1:T(8,128)(2,1)S(1)} fusion(f32[8,256,256]{1,2,0:T(8,128)} %copy-done.9, bf16[256,3,8,64]{0,3,2,1:T(8,128)(2,1)S(1)} %bitcast.104, f32[8,256,256]{1,2,0:T(8,128)} %get-tuple-element.23, f32[8,256]{1,0:T(8,128)S(1)} %get-tuple-element.22), kind=kOutput, calls=%fused_computation.38 | convolution fusion | flops 70912256 | bytes 8929280 | tf_op jit(solution)/shard_map/hqk,qhd->khd/dot_general | solution.py:137
  93.0 3.2 %fusion.70 = (f32[256]{0:T(256)S(1)}, f32[256]{0:T(256)S(1)}, f32[256,1024]{1,0:T(8,128)S(1)}) fusion(f32[256]{0:T(256)S(1)} %add_rsqrt_fusion, f32[256]{0:T(256)S(1)} %broadcast_multiply_fusion.2, bf16[256,1024]{1,0:T(8,128)(2,1)S(1)} %copy-done.6, bf16[256,1536]{0,1:T(8,128)(2,1)S(1)} %bitcast.91, bf16[1024,1536]{1,0:T(8,128)(2,1)} %bitcast.93), kind=kOutput, calls=%fused_computation.140 | convolution fusion | flops 806878720 | bytes 5509120 | tf_op jit(solution)/shard_map/dot_general | solution.py:142
  97.6 3.7 %fusion.75 = f32[16,64,1536]{2,1,0:T(8,128)} fusion(bf16[16,64,256]{2,1,0:T(8,128)(2,1)S(1)} %bitcast.100, bf16[256,1536,1]{0,1,2:T(8,128)(2,1)S(1)} %bitcast.92), kind=kOutput, calls=%fused_computation.143 | convolution fusion | flops 805306368 | bytes 7602176 | tf_op jit(solution)/shard_map/dot_general | solution.py:140
  101.3 3.5 %gather_fusion.3 = bf16[8,64,1536]{2,1,0:T(8,128)(2,1)S(1)} fusion(f32[16,64,1536]{2,1,0:T(8,128)} %fusion.75, s32[1024]{0:T(1024)S(1)} %pad_clamp_fusion), kind=kCustom, calls=%fused_computation.2.clone | custom fusion | bytes 3145760 | tf_op jit(solution)/shard_map/jit(_take)/gather | solution.py:67
  104.8 1.6 select_convert_fusion
  109.1 1.6 gather_fusion.4
  110.7 3.5 %gather_fusion.2 = f32[8,64,1536]{2,1,0:T(8,128)S(1)} fusion(f32[16,64,1536]{2,1,0:T(8,128)} %fusion.75, s32[1024]{0:T(1024)S(1)} %pad_clamp_fusion.1), kind=kCustom, calls=%fused_computation.clone | custom fusion | bytes 6291488 | tf_op jit(solution)/shard_map/jit(_take)/gather | solution.py:66
  114.5 3.2 %collective-permute-start.12 = (bf16[256,1024]{1,0:T(8,128)(2,1)}, bf16[256,1024]{1,0:T(8,128)(2,1)S(1)}, u32[]{:S(2)}, u32[]{:S(2)}) collective-permute-start(bf16[256,1024]{1,0:T(8,128)(2,1)} %get-tuple-element.17), channel_id=1, source_target_pairs={{7,0},{0,1},{1,2},{2,3},{3,4},{4,5},{5,6},{6,7},{15,8},{8,9},{9,10... | collective-permute-start | bytes 1572872 | tf_op jit(solution)/shard_map/ppermute | solution.py:38
  119.1 2.1 %select_add_fusion = f32[8,64,1536]{2,1,0:T(8,128)S(1)} fusion(f32[8,64,1536]{2,1,0:T(8,128)S(1)} %gather_fusion.2, bf16[8,64,1536]{2,1,0:T(8,128)(2,1)} %collective-permute-done.13, pred[8]{0:T(512)(128)(4,1)S(1)} %get-tuple-element.10), kind=kLoop, calls=%fused_computation.10 | loop fusion | flops 2359296 | bytes 7864328 | tf_op jit(solution)/shard_map/add | solution.py:68
  121.2 2.7 %collective-permute-start.14 = (bf16[4,64,1536]{2,1,0:T(8,128)(2,1)S(1)}, bf16[4,64,1536]{2,1,0:T(8,128)(2,1)S(1)}, u32[]{:S(2)}, u32[]{:S(2)}) collective-permute-start(bf16[4,64,1536]{2,1,0:T(8,128)(2,1)S(1)} %slice.138), channel_id=1, source_target_pairs={{0,2},{1,3},{2,0},{3,1},{4,6},{5,7},{6,4},{7,5},{8,9},{9,8},{10,11... | collective-permute-start | bytes 2359304 | tf_op jit(solution)/shard_map/ppermute | solution.py:30
  124.3 2.1 %collective-permute-done.6 = bf16[256,512]{0,1:T(8,128)(2,1)S(1)} collective-permute-done((bf16[256,512]{0,1:T(8,128)(2,1)S(1)}, bf16[256,512]{0,1:T(8,128)(2,1)S(1)}, u32[]{:S(2)}, u32[]{:S(2)}) %collective-permute-start.6) | collective-permute-done | bytes 262176 | tf_op jit(solution)/shard_map/ppermute | solution.py:38
  127.7 9.1 %collective-permute-done.18 = bf16[4,32,1024]{2,1,0:T(8,128)(2,1)S(1)} collective-permute-done((bf16[4,32,1024]{2,1,0:T(8,128)(2,1)S(1)}, bf16[4,32,1024]{2,1,0:T(8,128)(2,1)S(1)}, u32[]{:S(2)}, u32[]{:S(2)}) %collective-permute-start.18) | collective-permute-done | bytes 262176 | tf_op jit(solution)/shard_map/ppermute | solution.py:30
  136.8 12.4 %collective-permute-start.19 = (bf16[2,32,1024]{2,1,0:T(8,128)(2,1)S(1)}, bf16[2,32,1024]{2,1,0:T(8,128)(2,1)S(1)}, u32[]{:S(2)}, u32[]{:S(2)}) collective-permute-start(bf16[2,32,1024]{2,1,0:T(8,128)(2,1)S(1)} %slice.142), channel_id=1, source_target_pairs={{0,1},{1,0},{2,3},{3,2},{4,5},{5,4},{6,7},{7,6},{8,10},{9,11},{10,... | collective-permute-start | bytes 393224 | tf_op jit(solution)/shard_map/ppermute | solution.py:30
  150.5 1.6 collective-permute-done.19
  152.2 1.6 collective-permute-start.20
  153.8 3.5 %collective-permute-done.15 = bf16[2,64,1536]{2,1,0:T(8,128)(2,1)S(1)} collective-permute-done((bf16[2,64,1536]{2,1,0:T(8,128)(2,1)S(1)}, bf16[2,64,1536]{2,1,0:T(8,128)(2,1)S(1)}, u32[]{:S(2)}, u32[]{:S(2)}) %collective-permute-start.15) | collective-permute-done | bytes 393248 | tf_op jit(solution)/shard_map/ppermute | solution.py:30
  157.5 1.6 collective-permute-start.16
  159.7 10.0 %collective-permute-done.16 = bf16[1,64,1536]{2,1,0:T(8,128)(2,1)S(1)} collective-permute-done((bf16[1,64,1536]{2,1,0:T(8,128)(2,1)S(1)}, bf16[1,64,1536]{2,1,0:T(8,128)(2,1)S(1)}, u32[]{:S(2)}, u32[]{:S(2)}) %collective-permute-start.16) | collective-permute-done | bytes 196640 | tf_op jit(solution)/shard_map/ppermute | solution.py:30
  (133 shorter events, 39.7 us)
Async XLA Ops:
  0.6 45.7 %copy-start.8 = (bf16[64,1536]{1,0:T(8,128)(2,1)S(1)}, bf16[64,1536]{1,0:T(8,128)(2,1)}, u32[]{:S(2)}) copy-start(bf16[64,1536]{1,0:T(8,128)(2,1)} %param.15) | copy-start | bytes 589828
  1.5 19.7 %collective-permute-start.5 = (bf16[256,1]{0,1:T(2,128)(2,1)S(1)}, bf16[256,1]{0,1:T(2,128)(2,1)S(1)}, u32[]{:S(2)}, u32[]{:S(2)}) collective-permute-start(bf16[256,1]{0,1:T(2,128)(2,1)S(1)} %reshape.247), channel_id=1, source_target_pairs={{1,0},{2,1},{3,2},{4,3},{5,4},{6,5},{7,6},{0,7},{9,8},{10,9},{11,1... | collective-permute-start | bytes 1544 | tf_op jit(solution)/shard_map/ppermute | solution.py:38
  7.5 14.5 %collective-permute-start.7 = (bf16[1,32,1024]{2,1,0:T(8,128)(2,1)}, bf16[1,32,1024]{2,1,0:T(8,128)(2,1)S(1)}, u32[]{:S(2)}, u32[]{:S(2)}) collective-permute-start(bf16[1,32,1024]{2,1,0:T(8,128)(2,1)} %bitcast.108), channel_id=1, source_target_pairs={{0,4},{1,5},{2,6},{3,7},{4,0},{5,1},{6,2},{7,3},{8,12},{9,13},{10,... | collective-permute-start | bytes 196616 | tf_op jit(solution)/shard_map/ppermute | solution.py:30
  7.5 16.7 %collective-permute-start.1 = (bf16[1,64,1536]{2,1,0:T(8,128)(2,1)}, bf16[1,64,1536]{2,1,0:T(8,128)(2,1)S(1)}, u32[]{:S(2)}, u32[]{:S(2)}) collective-permute-start(bf16[1,64,1536]{2,1,0:T(8,128)(2,1)} %bitcast.94), channel_id=1, source_target_pairs={{0,4},{1,5},{2,6},{3,7},{4,0},{5,1},{6,2},{7,3},{8,12},{9,13},{10,... | collective-permute-start | bytes 589832 | tf_op jit(solution)/shard_map/ppermute | solution.py:30
  10.4 54.4 %collective-permute-start.11 = (bf16[256,1024]{1,0:T(8,128)(2,1)}, bf16[256,1024]{1,0:T(8,128)(2,1)S(1)}, u32[]{:S(2)}, u32[]{:S(2)}) collective-permute-start(bf16[256,1024]{1,0:T(8,128)(2,1)} %bitcast.115), channel_id=1, source_target_pairs={{1,0},{2,1},{3,2},{4,3},{5,4},{6,5},{7,6},{0,7},{9,8},{10,9},{11,1... | collective-permute-start | bytes 1572872 | tf_op jit(solution)/shard_map/ppermute | solution.py:38
  10.9 43.4 %collective-permute-start = (bf16[256,1024]{1,0:T(8,128)(2,1)}, bf16[256,1024]{1,0:T(8,128)(2,1)S(1)}, u32[]{:S(2)}, u32[]{:S(2)}) collective-permute-start(bf16[256,1024]{1,0:T(8,128)(2,1)} %bitcast.98), channel_id=1, source_target_pairs={{1,0},{2,1},{3,2},{4,3},{5,4},{6,5},{7,6},{0,7},{9,8},{10,9},{11,1... | collective-permute-start | bytes 1572872 | tf_op jit(solution)/shard_map/ppermute | solution.py:38
  17.4 36.0 %copy-start.13 = (bf16[32,1024]{1,0:T(8,128)(2,1)S(1)}, bf16[32,1024]{1,0:T(8,128)(2,1)}, u32[]{:S(2)}) copy-start(bf16[32,1024]{1,0:T(8,128)(2,1)} %param.16) | copy-start | bytes 196612
  22.9 14.2 %collective-permute-start.8 = (bf16[2,32,1024]{2,1,0:T(8,128)(2,1)S(1)}, bf16[2,32,1024]{2,1,0:T(8,128)(2,1)S(1)}, u32[]{:S(2)}, u32[]{:S(2)}) collective-permute-start(bf16[2,32,1024]{2,1,0:T(8,128)(2,1)S(1)} %pad_maximum_fusion.6), channel_id=1, source_target_pairs={{0,1},{1,0},{2,3},{3,2},{4,5},{5,4},{6,7},{7,6},{8,10},{9,11},{10,... | collective-permute-start | bytes 393224 | tf_op jit(solution)/shard_map/ppermute | solution.py:30
  25.1 29.2 %copy-start.10 = (bf16[1,16,16,1024]{3,2,1,0:T(8,128)(2,1)S(1)}, bf16[1,16,16,1024]{3,2,1,0:T(8,128)(2,1)}, u32[]{:S(2)}) copy-start(bf16[1,16,16,1024]{3,2,1,0:T(8,128)(2,1)} %param.12) | copy-start | bytes 1572868
  25.2 21.2 %collective-permute-start.2 = (bf16[2,64,1536]{2,1,0:T(8,128)(2,1)S(1)}, bf16[2,64,1536]{2,1,0:T(8,128)(2,1)S(1)}, u32[]{:S(2)}, u32[]{:S(2)}) collective-permute-start(bf16[2,64,1536]{2,1,0:T(8,128)(2,1)S(1)} %pad_maximum_fusion.4), channel_id=1, source_target_pairs={{0,1},{1,0},{2,3},{3,2},{4,5},{5,4},{6,7},{7,6},{8,10},{9,11},{10,... | collective-permute-start | bytes 1179656 | tf_op jit(solution)/shard_map/ppermute | solution.py:30
  37.9 15.6 %collective-permute-start.9 = (bf16[4,32,1024]{2,1,0:T(8,128)(2,1)S(1)}, bf16[4,32,1024]{2,1,0:T(8,128)(2,1)S(1)}, u32[]{:S(2)}, u32[]{:S(2)}) collective-permute-start(bf16[4,32,1024]{2,1,0:T(8,128)(2,1)S(1)} %pad_maximum_fusion.5), channel_id=1, source_target_pairs={{0,2},{1,3},{2,0},{3,1},{4,6},{5,7},{6,4},{7,5},{8,9},{9,8},{10,11... | collective-permute-start | bytes 786440 | tf_op jit(solution)/shard_map/ppermute | solution.py:30
  46.4 17.0 %collective-permute-start.3 = (bf16[4,64,1536]{2,1,0:T(8,128)(2,1)S(1)}, bf16[4,64,1536]{2,1,0:T(8,128)(2,1)S(1)}, u32[]{:S(2)}, u32[]{:S(2)}) collective-permute-start(bf16[4,64,1536]{2,1,0:T(8,128)(2,1)S(1)} %pad_maximum_fusion.1), channel_id=1, source_target_pairs={{0,2},{1,3},{2,0},{3,1},{4,6},{5,7},{6,4},{7,5},{8,9},{9,8},{10,11... | collective-permute-start | bytes 2359304 | tf_op jit(solution)/shard_map/ppermute | solution.py:30
  53.5 12.3 %collective-permute-start.10 = (bf16[8,32,1024]{2,1,0:T(8,128)(2,1)S(1)}, bf16[8,32,1024]{2,1,0:T(8,128)(2,1)S(1)}, u32[]{:S(2)}, u32[]{:S(2)}) collective-permute-start(bf16[8,32,1024]{2,1,0:T(8,128)(2,1)S(1)} %pad_maximum_fusion.3), channel_id=1, source_target_pairs={{0,8},{8,0},{1,9},{9,1},{2,10},{10,2},{3,11},{11,3},{4,12},{12,4},... | collective-permute-start | bytes 1572872 | tf_op jit(solution)/shard_map/ppermute | solution.py:34
  54.7 10.1 %copy-start.14 = (bf16[1,16,16,1024]{3,2,1,0:T(8,128)(2,1)S(1)}, bf16[1,16,16,1024]{3,2,1,0:T(8,128)(2,1)}, u32[]{:S(2)}) copy-start(bf16[1,16,16,1024]{3,2,1,0:T(8,128)(2,1)} %param.17) | copy-start | bytes 1572868
  64.8 6.6 %collective-permute-start.4 = (bf16[8,64,1536]{2,1,0:T(8,128)(2,1)}, bf16[8,64,1536]{2,1,0:T(8,128)(2,1)}, u32[]{:S(2)}, u32[]{:S(2)}) collective-permute-start(bf16[8,64,1536]{2,1,0:T(8,128)(2,1)} %pad_maximum_fusion), channel_id=1, source_target_pairs={{0,8},{8,0},{1,9},{9,1},{2,10},{10,2},{3,11},{11,3},{4,12},{12,4},... | collective-permute-start | bytes 4718600 | tf_op jit(solution)/shard_map/ppermute | solution.py:34
  65.0 3.8 %copy-start.2 = (bf16[256,1024]{1,0:T(8,128)(2,1)}, bf16[256,1024]{1,0:T(8,128)(2,1)S(1)}, u32[]{:S(2)}) copy-start(bf16[256,1024]{1,0:T(8,128)(2,1)S(1)} %broadcast_select_fusion.2) | copy-start | bytes 1572868
  88.6 4.4 %copy-start.6 = (bf16[256,1024]{1,0:T(8,128)(2,1)S(1)}, bf16[256,1024]{1,0:T(8,128)(2,1)}, u32[]{:S(2)}) copy-start(bf16[256,1024]{1,0:T(8,128)(2,1)} %copy-done.4) | copy-start | bytes 1572868
  93.0 3.2 %copy-start.3 = (bf16[256,1024]{1,0:T(8,128)(2,1)S(1)}, bf16[256,1024]{1,0:T(8,128)(2,1)}, u32[]{:S(2)}) copy-start(bf16[256,1024]{1,0:T(8,128)(2,1)} %copy-done.2) | copy-start | bytes 1572868
  106.4 12.7 %collective-permute-start.13 = (bf16[8,64,1536]{2,1,0:T(8,128)(2,1)}, bf16[8,64,1536]{2,1,0:T(8,128)(2,1)}, u32[]{:S(2)}, u32[]{:S(2)}) collective-permute-start(bf16[8,64,1536]{2,1,0:T(8,128)(2,1)} %select_convert_fusion), channel_id=1, source_target_pairs={{0,8},{8,0},{1,9},{9,1},{2,10},{10,2},{3,11},{11,3},{4,12},{12,4},... | collective-permute-start | bytes 4718600 | tf_op jit(solution)/shard_map/ppermute | solution.py:34
  114.2 12.2 %collective-permute-start.6 = (bf16[256,512]{0,1:T(8,128)(2,1)S(1)}, bf16[256,512]{0,1:T(8,128)(2,1)S(1)}, u32[]{:S(2)}, u32[]{:S(2)}) collective-permute-start(bf16[256,512]{0,1:T(8,128)(2,1)S(1)} %bitcast.113), channel_id=1, source_target_pairs={{7,0},{0,1},{1,2},{2,3},{3,4},{4,5},{5,6},{6,7},{15,8},{8,9},{9,10... | collective-permute-start | bytes 786440 | tf_op jit(solution)/shard_map/ppermute | solution.py:38
  114.5 35.0 %collective-permute-start.12 = (bf16[256,1024]{1,0:T(8,128)(2,1)}, bf16[256,1024]{1,0:T(8,128)(2,1)S(1)}, u32[]{:S(2)}, u32[]{:S(2)}) collective-permute-start(bf16[256,1024]{1,0:T(8,128)(2,1)} %get-tuple-element.17), channel_id=1, source_target_pairs={{7,0},{0,1},{1,2},{2,3},{3,4},{4,5},{5,6},{6,7},{15,8},{8,9},{9,10... | collective-permute-start | bytes 1572872 | tf_op jit(solution)/shard_map/ppermute | solution.py:38
  119.0 5.0 %collective-permute-start.17 = (bf16[8,32,1024]{2,1,0:T(8,128)(2,1)S(1)}, bf16[8,32,1024]{2,1,0:T(8,128)(2,1)S(1)}, u32[]{:S(2)}, u32[]{:S(2)}) collective-permute-start(bf16[8,32,1024]{2,1,0:T(8,128)(2,1)S(1)} %select_convert_fusion.1), channel_id=1, source_target_pairs={{0,8},{8,0},{1,9},{9,1},{2,10},{10,2},{3,11},{11,3},{4,12},{12,4},... | collective-permute-start | bytes 1572872 | tf_op jit(solution)/shard_map/ppermute | solution.py:34
  119.0 4.9 %copy-start.7 = (f32[8,32,1024]{2,1,0:T(8,128)S(1)}, f32[8,32,1024]{2,1,0:T(8,128)}, u32[]{:S(2)}) copy-start(f32[8,32,1024]{2,1,0:T(8,128)} %gather_fusion.4) | copy-start | bytes 3145732
  121.1 5.2 %copy-start.1 = (bf16[512,1024]{1,0:T(8,128)(2,1)S(1)}, bf16[512,1024]{1,0:T(8,128)(2,1)}, u32[]{:S(2)}) copy-start(bf16[512,1024]{1,0:T(8,128)(2,1)} %copy-done) | copy-start | bytes 3145732
  121.1 5.2 %copy-start.11 = (bf16[1,16,16,1024]{3,2,1,0:T(8,128)(2,1)S(1)}, bf16[1,16,16,1024]{3,2,1,0:T(8,128)(2,1)}, u32[]{:S(2)}) copy-start(bf16[1,16,16,1024]{3,2,1,0:T(8,128)(2,1)} %param.12) | copy-start | bytes 1572868
  121.2 28.0 %collective-permute-start.14 = (bf16[4,64,1536]{2,1,0:T(8,128)(2,1)S(1)}, bf16[4,64,1536]{2,1,0:T(8,128)(2,1)S(1)}, u32[]{:S(2)}, u32[]{:S(2)}) collective-permute-start(bf16[4,64,1536]{2,1,0:T(8,128)(2,1)S(1)} %slice.138), channel_id=1, source_target_pairs={{0,2},{1,3},{2,0},{3,1},{4,6},{5,7},{6,4},{7,5},{8,9},{9,8},{10,11... | collective-permute-start | bytes 2359304 | tf_op jit(solution)/shard_map/ppermute | solution.py:30
  124.2 12.5 %collective-permute-start.18 = (bf16[4,32,1024]{2,1,0:T(8,128)(2,1)S(1)}, bf16[4,32,1024]{2,1,0:T(8,128)(2,1)S(1)}, u32[]{:S(2)}, u32[]{:S(2)}) collective-permute-start(bf16[4,32,1024]{2,1,0:T(8,128)(2,1)S(1)} %slice.140), channel_id=1, source_target_pairs={{0,2},{1,3},{2,0},{3,1},{4,6},{5,7},{6,4},{7,5},{8,9},{9,8},{10,11... | collective-permute-start | bytes 786440 | tf_op jit(solution)/shard_map/ppermute | solution.py:30
  136.8 12.8 %copy-start.12 = (bf16[256,1024]{1,0:T(8,128)(2,1)S(1)}, bf16[256,1024]{1,0:T(8,128)(2,1)}, u32[]{:S(2)}) copy-start(bf16[256,1024]{1,0:T(8,128)(2,1)} %get-tuple-element.17) | copy-start | bytes 1572868
  136.8 15.3 %collective-permute-start.19 = (bf16[2,32,1024]{2,1,0:T(8,128)(2,1)S(1)}, bf16[2,32,1024]{2,1,0:T(8,128)(2,1)S(1)}, u32[]{:S(2)}, u32[]{:S(2)}) collective-permute-start(bf16[2,32,1024]{2,1,0:T(8,128)(2,1)S(1)} %slice.142), channel_id=1, source_target_pairs={{0,1},{1,0},{2,3},{3,2},{4,5},{5,4},{6,7},{7,6},{8,10},{9,11},{10,... | collective-permute-start | bytes 393224 | tf_op jit(solution)/shard_map/ppermute | solution.py:30
  149.5 7.8 %collective-permute-start.15 = (bf16[2,64,1536]{2,1,0:T(8,128)(2,1)S(1)}, bf16[2,64,1536]{2,1,0:T(8,128)(2,1)S(1)}, u32[]{:S(2)}, u32[]{:S(2)}) collective-permute-start(bf16[2,64,1536]{2,1,0:T(8,128)(2,1)S(1)} %slice.139), channel_id=1, source_target_pairs={{0,1},{1,0},{2,3},{3,2},{4,5},{5,4},{6,7},{7,6},{8,10},{9,11},{10,... | collective-permute-start | bytes 1179656 | tf_op jit(solution)/shard_map/ppermute | solution.py:30
  152.2 6.8 %collective-permute-start.20 = (bf16[1,32,1024]{2,1,0:T(8,128)(2,1)S(1)}, bf16[1,32,1024]{2,1,0:T(8,128)(2,1)S(1)}, u32[]{:S(2)}, u32[]{:S(2)}) collective-permute-start(bf16[1,32,1024]{2,1,0:T(8,128)(2,1)S(1)} %slice.143), channel_id=1, source_target_pairs={{0,4},{1,5},{2,6},{3,7},{4,0},{5,1},{6,2},{7,3},{8,12},{9,13},{10,... | collective-permute-start | bytes 196616 | tf_op jit(solution)/shard_map/ppermute | solution.py:30
  157.5 12.3 %collective-permute-start.16 = (bf16[1,64,1536]{2,1,0:T(8,128)(2,1)S(1)}, bf16[1,64,1536]{2,1,0:T(8,128)(2,1)S(1)}, u32[]{:S(2)}, u32[]{:S(2)}) collective-permute-start(bf16[1,64,1536]{2,1,0:T(8,128)(2,1)S(1)} %slice.141), channel_id=1, source_target_pairs={{0,4},{1,5},{2,6},{3,7},{4,0},{5,1},{6,2},{7,3},{8,12},{9,13},{10,... | collective-permute-start | bytes 589832 | tf_op jit(solution)/shard_map/ppermute | solution.py:30
  (6 other events, 8.8 us)

commit v2 on v1

v2 whole, which is shorter than its diff:
```python
import functools

import jax
import jax.numpy as jnp
import numpy as np
from jax import lax
from jax.experimental import pallas as pl
from jax.experimental.pallas import tpu as pltpu
from jax.sharding import PartitionSpec as P

HEADS = 8
HD = 64
PAIR = 2 * HD
F32 = jnp.float32
BF16 = jnp.bfloat16
VM = pl.BlockSpec(memory_space=pltpu.VMEM)
SM = pl.BlockSpec(memory_space=pltpu.SMEM)


def stage_masks(rows):
    bits = [1 << b for b in range(rows.bit_length() - 1)]
    far = bits[:1:-1]
    return (far + bits[:2], far + bits[:2][::-1])


def slot_masks(rows, core):
    masks = [0]
    for m in stage_masks(rows)[core]:
        masks = masks + [a ^ m for a in masks]
    return np.array(masks, np.int32)


def exchange(block, rows, stage):
    masks = stage_masks(rows)
    pairs = [
        (c * rows + i, c * rows + (i ^ masks[c][stage])) for c in range(2) for i in range(rows)
    ]
    return lax.ppermute(block, ("fsdp", "rows"), pairs)


def swap_cores(block):
    return lax.ppermute(block, "fsdp", [(0, 1), (1, 0)])


def shifted(block, rows, distance):
    return lax.ppermute(block, "rows", [((i - distance) % rows, i) for i in range(rows)])


def call(kernel, outs, specs, scratch=(), flops=0, moved=0, name=None):
    return pl.pallas_call(
        kernel,
        out_shape=tuple(jax.ShapeDtypeStruct(s, d) for s, d in outs),
        in_specs=list(specs),
        out_specs=tuple(VM for _ in outs),
        scratch_shapes=list(scratch),
        compiler_params=pltpu.CompilerParams(vmem_limit_bytes=40 << 20),
        cost_estimate=pl.CostEstimate(flops=flops, bytes_accessed=moved, transcendentals=0),
        name=name,
    )


def dot(a, b, ca=1, cb=0):
    return lax.dot_general(a, b, (((ca,), (cb,)), ((), ())), preferred_element_type=F32)


def place(dst, src, table, first, count, size):
    def step(j, carry):
        at = pl.multiple_of(table[first + j] * size, size)
        dst[pl.ds(at, size), :] = src[pl.ds(pl.multiple_of(j * size, size), size), :]
        return carry

    lax.fori_loop(0, count, step, 0)


def pick(dst, src, table, count, size):
    def step(j, carry):
        at = pl.multiple_of(table[j] * size, size)
        dst[pl.ds(pl.multiple_of(j * size, size), size), :] = src[pl.ds(at, size), :]
        return carry

    lax.fori_loop(0, count, step, 0)


def borrowed_rows(scal, low, count, cols, forward):
    row = (lax.broadcasted_iota(jnp.int32, (count, 1), 0) + low) // cols
    return row < scal[0] if forward else row >= scal[0]


def norm_kernel(scal, table, own, halo, xw, normed_bf, ordered, mean_out, inv_out, turned, *, low, cols, forward, blocks):
    half = halo.shape[0]
    take = borrowed_rows(scal, low, half, cols, forward)
    keep_low = half - low
    xw[pl.ds(keep_low, half), :] = own[pl.ds(keep_low, half), :]
    mixed = jnp.where(take, halo[...].astype(F32), own[pl.ds(low, half), :].astype(F32))
    xw[pl.ds(low, half), :] = mixed.astype(BF16)
    x = xw[...].astype(F32)
    mean = jnp.mean(x, axis=-1, keepdims=True)
    centered = x - mean
    inv = lax.rsqrt(jnp.mean(centered * centered, axis=-1, keepdims=True) + 1e-05)
    normed = centered * inv
    normed_bf[...] = normed.astype(BF16)
    mean_out[...] = mean
    inv_out[...] = inv
    turned[...] = normed.T.astype(BF16)
    pick(ordered, turned, table, blocks, turned.shape[0] // blocks)


def forward_kernel(place_at, order, normed_bf, bias, w0, w1, w2, w3, full, packed, attn, ctx, ctx_ordered, turned, *, blocks):
    size = full.shape[0] // blocks
    quarter = blocks // 4
    for i, w in enumerate((w0, w1, w2, w3)):
        place(full, w, place_at, i * quarter, quarter, size)
    hidden = ctx.shape[1]
    packed[...] = dot(normed_bf[...], full[...]).astype(BF16)
    cells = normed_bf.shape[0]
    first = lax.broadcasted_iota(jnp.int32, (cells, PAIR), 1) < HD
    for p in range(HEADS // 2):
        lanes = pl.ds(p * PAIR, PAIR)
        q = packed[:, lanes].astype(F32)
        k = packed[:, pl.ds(hidden + p * PAIR, PAIR)]
        v = packed[:, pl.ds(2 * hidden + p * PAIR, PAIR)]
        parts = []
        for side in range(2):
            q_one = jnp.where(first if side == 0 else ~first, q, 0.0).astype(BF16)
            scores = dot(q_one, k, 1, 1) * (HD ** (-0.5)) + bias[...]
            e = jnp.exp(scores - jnp.max(scores, axis=-1, keepdims=True))
            a = e * (1.0 / jnp.sum(e, axis=-1, keepdims=True))
            attn[2 * p + side] = a
            parts.append(dot(a.astype(BF16), v))
        both = jnp.where(first, parts[0], parts[1])
        ctx[:, lanes] = both.astype(BF16)
        turned[lanes, :] = both.T.astype(BF16)
    pick(ctx_ordered, turned, order, blocks, turned.shape[0] // blocks)


def term_out_kernel(scal, ctx_ordered, own, halo, cot, keep, send, *, low, cols, forward):
    half = halo.shape[0]
    take = borrowed_rows(scal, low, half, cols, forward)
    keep_low = half - low
    cot[pl.ds(keep_low, half), :] = own[pl.ds(keep_low, half), :]
    cot[pl.ds(low, half), :] = jnp.where(
        take, halo[...].astype(F32), own[pl.ds(low, half), :].astype(F32)
    ).astype(BF16)
    n = keep.shape[0]
    send[...] = dot(ctx_ordered[pl.ds(n, n), :], cot[...]).astype(BF16)
    keep[...] = dot(ctx_ordered[pl.ds(0, n), :], cot[...])


def backward_kernel(place_at, cot, packed, attn, ordered, w0, w1, w2, w3, full, gp, keep, send, gctx, *, blocks):
    size = full.shape[0] // blocks
    quarter = blocks // 4
    for i, w in enumerate((w0, w1, w2, w3)):
        place(full, w, place_at, i * quarter, quarter, size)
    hidden = full.shape[0]
    cells = cot.shape[0]
    gctx[...] = dot(cot[...], full[...], 1, 1).astype(BF16)
    first = lax.broadcasted_iota(jnp.int32, (cells, PAIR), 1) < HD
    for p in range(HEADS // 2):
        lanes = pl.ds(p * PAIR, PAIR)
        q = packed[:, lanes]
        k = packed[:, pl.ds(hidden + p * PAIR, PAIR)]
        v = packed[:, pl.ds(2 * hidden + p * PAIR, PAIR)]
        g = gctx[:, lanes]
        gf = g.astype(F32)
        gq, gk, gv = [], [], []
        for side in range(2):
            g_one = jnp.where(first if side == 0 else ~first, gf, 0.0).astype(BF16)
            a = attn[2 * p + side]
            ga = dot(g_one, v, 1, 1)
            inner = jnp.sum(ga * a, axis=-1, keepdims=True)
            gs = (a * (ga - inner) * (HD ** (-0.5))).astype(BF16)
            gq.append(dot(gs, k))
            gk.append(dot(gs, q, 0, 0))
            gv.append(dot(a.astype(BF16), g, 0, 0))
        gp[:, lanes] = jnp.where(first, gq[0], gq[1]).astype(BF16)
        gp[:, pl.ds(hidden + p * PAIR, PAIR)] = jnp.where(first, gk[0], gk[1]).astype(BF16)
        gp[:, pl.ds(2 * hidden + p * PAIR, PAIR)] = jnp.where(first, gv[0], gv[1]).astype(BF16)
    n = keep.shape[0]
    send[...] = dot(ordered[pl.ds(n, n), :], gp[...]).astype(BF16)
    keep[...] = dot(ordered[pl.ds(0, n), :], gp[...])


def grad_kernel(xw, mean, inv, gp, full, cot, grad):
    gn = dot(gp[...], full[...], 1, 1)
    normed = (xw[...].astype(F32) - mean[...]) * inv[...]
    m1 = jnp.mean(gn, axis=-1, keepdims=True)
    m2 = jnp.mean(gn * normed, axis=-1, keepdims=True)
    grad[...] = (cot[...].astype(F32) + inv[...] * (gn - m1 - normed * m2)).astype(BF16)


def output_kernel(scal, own, ctx, back, full, out, mixed, *, low, cols, forward):
    half = back.shape[0]
    take = borrowed_rows(scal, low, half, cols, forward)
    keep_low = half - low
    mixed[pl.ds(keep_low, half), :] = ctx[pl.ds(keep_low, half), :]
    mixed[pl.ds(low, half), :] = jnp.where(
        take, back[...].astype(F32), ctx[pl.ds(low, half), :].astype(F32)
    ).astype(BF16)
    out[...] = (own[...].astype(F32) + dot(mixed[...], full[...])).astype(BF16)


def gather_parts(shard, rows):
    stages = len(stage_masks(rows)[0])
    held = shard
    for stage in range(stages - 1):
        held = jnp.concatenate([held, exchange(held, rows, stage)], axis=0)
    last = exchange(held, rows, stages - 1)
    return held, last, swap_cores(held), swap_cores(last)


def scatter_parts(keep, send, rows):
    stages = len(stage_masks(rows)[0])
    keep = keep + swap_cores(send).astype(F32)
    for stage in range(stages - 1, -1, -1):
        half = keep.shape[0] // 2
        arrived = exchange(keep[half:].astype(BF16), rows, stage)
        keep = keep[:half] + arrived.astype(F32)
    return keep


def branch(tokens, cell_mask, shifts, projection_in, projection_out, cotangent, *, forward):
    rows = lax.axis_size("rows")
    row_count, cols, dim = tokens.shape[1:]
    cells = row_count * cols
    half = cells // 2
    hidden = HEADS * HD
    low = 0 if forward else half
    distance = -1 if forward else 1
    core = lax.axis_index("fsdp")
    me = lax.axis_index("rows")
    blocks = 2 * rows
    m0 = jnp.asarray(slot_masks(rows, 0))
    m1 = jnp.asarray(slot_masks(rows, 1))
    mine = jnp.where(core == 0, m0, m1) ^ me
    theirs = jnp.where(core == 0, m1, m0) ^ me
    table = jnp.concatenate([core * rows + mine, (1 - core) * rows + theirs]).astype(jnp.int32)
    scal = shifts.astype(jnp.int32)
    s_row, s_col = scal[0], scal[1]
    part = lambda a: lax.slice_in_dim(a, low, low + half, axis=0)

    own = tokens.reshape(cells, dim)
    own_cot = cotangent.reshape(cells, dim)
    own_mask = cell_mask.astype(BF16).reshape(cells, 1)
    halo = shifted(part(own), rows, distance)
    halo_mask = shifted(part(own_mask), rows, distance)
    in_parts = gather_parts(projection_in, rows)
    out_parts = gather_parts(projection_out, rows)
    halo_cot = shifted(part(own_cot), rows, distance)

    cell = jnp.arange(cells, dtype=jnp.int32)
    cell_row, cell_col = cell // cols, cell % cols
    from_other = (cell_row < s_row) if forward else (cell_row >= s_row)
    pad = ((low, half - low), (0, 0))
    key_ok = jnp.where(from_other, jnp.pad(halo_mask, pad)[:, 0], own_mask[:, 0]) > 0
    at_wrap = me == (rows - 1 if forward else 0)
    region = 2 * ((cell_row < s_row) & at_wrap).astype(jnp.int32) + (cell_col < s_col).astype(
        jnp.int32
    )
    allowed = (region[:, None] == region[None, :]) & (
        key_ok[None, :] | (cell[:, None] == cell[None, :])
    )
    bias = jnp.where(allowed, 0.0, -1e30).astype(F32)

    shape_kw = dict(low=low, cols=cols, forward=forward)
    xw, normed_bf, ordered, mean, inv = call(
        functools.partial(norm_kernel, blocks=blocks, **shape_kw),
        [((cells, dim), BF16), ((cells, dim), BF16), ((dim, cells), BF16), ((cells, 1), F32), ((cells, 1), F32)],
        [SM, SM, VM, VM],
        [pltpu.VMEM((dim, cells), BF16)],
        flops=20 * cells * dim,
        moved=10 * cells * dim,
        name="norm",
    )(scal, table, own, halo)
    full_in, packed, attn, ctx, ctx_ordered = call(
        functools.partial(forward_kernel, blocks=blocks),
        [((dim, 3 * hidden), BF16), ((cells, 3 * hidden), BF16), ((HEADS, cells, cells), F32), ((cells, hidden), BF16), ((hidden, cells), BF16)],
        [SM, SM, VM, VM, VM, VM, VM, VM],
        [pltpu.VMEM((hidden, cells), BF16)],
        flops=6 * cells * dim * 3 * hidden,
        moved=10 << 20,
        name="fwd",
    )(table, table, normed_bf, bias, *in_parts)
    back_ctx = shifted(part(ctx), rows, -distance)
    cot, keep_out, send_out = call(
        functools.partial(term_out_kernel, **shape_kw),
        [((cells, dim), BF16), ((hidden // 2, dim), F32), ((hidden // 2, dim), BF16)],
        [SM, VM, VM, VM],
        flops=2 * cells * dim * hidden,
        moved=4 << 20,
        name="term_out",
    )(scal, ctx_ordered, own_cot, halo_cot)
    grad_out = scatter_parts(keep_out, send_out, rows)
    full_out, gp, keep_in, send_in = call(
        functools.partial(backward_kernel, blocks=blocks),
        [((hidden, dim), BF16), ((cells, 3 * hidden), BF16), ((dim // 2, 3 * hidden), F32), ((dim // 2, 3 * hidden), BF16)],
        [SM, VM, VM, VM, VM, VM, VM, VM, VM],
        [pltpu.VMEM((cells, hidden), BF16)],
        flops=8 * cells * dim * 3 * hidden,
        moved=12 << 20,
        name="bwd",
    )(table, cot, packed, attn, ordered, *out_parts)
    grad_in = scatter_parts(keep_in, send_in, rows)
    (grad_win,) = call(
        grad_kernel,
        [((cells, dim), BF16)],
        [VM] * 6,
        flops=2 * cells * dim * 3 * hidden,
        moved=6 << 20,
        name="grad",
    )(xw, mean, inv, gp, full_in, cot)
    back_grad = shifted(part(grad_win), rows, -distance)
    (output,) = call(
        functools.partial(output_kernel, **shape_kw),
        [((cells, dim), BF16)],
        [SM, VM, VM, VM, VM],
        [pltpu.VMEM((cells, hidden), BF16)],
        flops=2 * cells * dim * hidden,
        moved=3 << 20,
        name="output",
    )(scal, own, ctx, back_ctx, full_out)
    own_grad = jnp.where(from_other[:, None], jnp.pad(back_grad, pad), grad_win)
    shape = tokens.shape
    return (output.reshape(shape), own_grad.reshape(shape), grad_in, grad_out)


def body(tokens, cell_mask, shifts, projection_in, projection_out, cotangent):
    return lax.cond(
        shifts[0] <= tokens.shape[1] // 2,
        functools.partial(branch, forward=True),
        functools.partial(branch, forward=False),
        tokens, cell_mask, shifts, projection_in, projection_out, cotangent,
    )


def solution(mesh):
    placed = (
        P(("groups", "fsdp"), "rows", None, None),
        P(("groups", "fsdp"), "rows", None),
        P(),
        P(("fsdp", "rows"), None),
        P(("fsdp", "rows"), None),
        P(("groups", "fsdp"), "rows", None, None),
    )
    return jax.shard_map(
        body,
        mesh=mesh,
        in_specs=placed,
        out_specs=(
            P(("groups", "fsdp"), "rows", None, None),
            P(("groups", "fsdp"), "rows", None, None),
            P(("groups", "fsdp", "rows"), None),
            P(("groups", "fsdp", "rows"), None),
        ),
        check_vma=False,
    )
```

time: 171 us -> 119 us (0.70)
  local copies, waits for them, and re-layouts: 31.9 us -> 3.06 us
  matrix products: 20.8 us -> 0 us
  other arithmetic: 22.5 us -> 7.18 us
  Pallas kernels: 0 us -> 14.8 us
  starting transfers between devices: 49.8 us -> 45.1 us
  waiting for transfers between devices: 44.4 us -> 46.8 us
    dot_general x11 -> x0, matrix products: 18.6 us -> none  [the longest x1 4.25 us: body(): gk = jnp.einsum('hqk,qhd->khd', grad_scores, q, preferred_element_type=f32)]
    pallas_call x0 -> x6, Pallas kernels: none -> 14.8 us  [the longest x1 5.15 us: branch(): call(functools.partial(backward_kernel, blocks=blocks), [((hidden, dim),...]
    gather x6 -> x0, local copies, waits for them, and re-layouts: 14.5 us -> none  [the longest x2 5.14 us: scatter_rows(): keep = jnp.take(blocks, core * rows + own, axis=0)]
    unnamed x42 -> x0, local copies, waits for them, and re-layouts: 11.3 us -> none
    ppermute x12, waiting for transfers between devices: 42.4 us -> 33.9 us  [exchange(): return lax.ppermute(block, ('fsdp', 'rows'), pairs)]
    ppermute x5, waiting for transfers between devices: 2.07 us -> 9.92 us  [shifted(): lax.ppermute(block, 'rows', [((i - distance) % rows, i) for i in range(ro...]
    ppermute x12, starting transfers between devices: 37.7 us -> 33.2 us  [exchange(): return lax.ppermute(block, ('fsdp', 'rows'), pairs)]
    convert_element_type x3 -> x1, other arithmetic: 3.54 us -> 0.01 us  [branch(): own_mask = cell_mask.astype(BF16).reshape(cells, 1)]
  transfers between devices with their start and end apart: 21 -> 23, of which waited for: 7 -> 11; matrix products, arithmetic and copies ran while one was open for 22% -> 7% of each run, Pallas kernels for 0% -> 8%
where the time goes in v2:
time: 119 us
  waiting for transfers between devices  46.8 us (39%)
  starting transfers between devices  45.1 us (38%)
  Pallas kernels  14.8 us (12%)
  other arithmetic  7.18 us (6%)
  local copies, waits for them, and re-layouts  3.06 us (3%)
  between operations  1.28 us (1%)
    ppermute x12, waiting for transfers between devices, exchange(): return lax.ppermute(block, ('fsdp', 'rows'), pairs)  33.9 us
    ppermute x12, starting transfers between devices, exchange(): return lax.ppermute(block, ('fsdp', 'rows'), pairs)  33.2 us
    ppermute x5, starting transfers between devices, shifted(): lax.ppermute(block, 'rows', [((i - distance) % rows, i) for i in range(ro...  10.5 us
    ppermute x5, waiting for transfers between devices, shifted(): lax.ppermute(block, 'rows', [((i - distance) % rows, i) for i in range(ro...  9.92 us
    pallas_call x1, Pallas kernels, branch(): call(functools.partial(backward_kernel, blocks=blocks), [((hidden, dim),...  5.15 us
    pallas_call x1, Pallas kernels, branch(): call(functools.partial(forward_kernel, blocks=blocks), [((dim, 3 * hidden...  3.88 us
    ppermute x6, waiting for transfers between devices, swap_cores(): return lax.ppermute(block, 'fsdp', [(0, 1), (1, 0)])  2.91 us
  transfers between devices with their start and end apart: 23, of which 11 were waited for; matrix products, arithmetic and copies ran while one was open for 7% of the time, Pallas kernels for 8%

profile of v2, /device:TPU:0, one launch (start us, length us, event | category | flops | bytes accessed | tf_op | source)
XLA Modules:
  0.0 118.5 jit_solution(16755628590562804008)
XLA Ops:
  1.3 117.2 %conditional.1 = (bf16[1,16,16,1024]{3,2,1,0:T(8,128)(2,1)}, bf16[1,16,16,1024]{3,2,1,0:T(8,128)(2,1)}, f32[64,1536]{1,0:T(8,128)}, f32[32,1024]{1,0:T(8,128)}) conditional(s32[]{:T(128)} %bitcast.16, (bf16[1,16,16,1024]{3,2,1,0:T(8,128)(2,1)}, s32[8]{0:T(128)}, s32[8]{0:T(128)}, s32[2]{0:T(128)}, s32[1,16,16]{2,1,0:T(8,128)}, ...), branch_computations={%region_0.1_spmd, %region_1.2_spmd} | conditional | flops 6990145536 | bytes 110902352 | solution.py:327
  1.4 4.1 %collective-permute-start.2 = (bf16[64,1536]{1,0:T(8,128)(2,1)}, bf16[64,1536]{1,0:T(8,128)(2,1)S(1)}, u32[]{:S(2)}, u32[]{:S(2)}) collective-permute-start(bf16[64,1536]{1,0:T(8,128)(2,1)} %get-tuple-element.38), channel_id=1, source_target_pairs={{0,4},{1,5},{2,6},{3,7},{4,0},{5,1},{6,2},{7,3},{8,12},{9,13},{10,... | collective-permute-start | bytes 589832 | tf_op jit(solution)/shard_map/cond/branch_0_fun/ppermute | solution.py:38
  5.5 9.3 %collective-permute-done.2 = bf16[64,1536]{1,0:T(8,128)(2,1)S(1)} collective-permute-done((bf16[64,1536]{1,0:T(8,128)(2,1)}, bf16[64,1536]{1,0:T(8,128)(2,1)S(1)}, u32[]{:S(2)}, u32[]{:S(2)}) %collective-permute-start.2) | collective-permute-done | bytes 196640 | tf_op jit(solution)/shard_map/cond/branch_0_fun/ppermute | solution.py:38
  15.7 1.6 %collective-permute-start.3 = (bf16[128,1536]{1,0:T(8,128)(2,1)S(1)}, bf16[128,1536]{1,0:T(8,128)(2,1)S(1)}, u32[]{:S(2)}, u32[]{:S(2)}) collective-permute-start(bf16[128,1536]{1,0:T(8,128)(2,1)S(1)} %pad_maximum_fusion), channel_id=1, source_target_pairs={{0,1},{1,0},{2,3},{3,2},{4,5},{5,4},{6,7},{7,6},{8,10},{9,11},{10,... | collective-permute-start | bytes 1179656 | tf_op jit(solution)/shard_map/cond/branch_0_fun/ppermute | solution.py:38
  18.3 5.2 %collective-permute-done.3 = bf16[128,1536]{1,0:T(8,128)(2,1)S(1)} collective-permute-done((bf16[128,1536]{1,0:T(8,128)(2,1)S(1)}, bf16[128,1536]{1,0:T(8,128)(2,1)S(1)}, u32[]{:S(2)}, u32[]{:S(2)}) %collective-permute-start.3) | collective-permute-done | bytes 393248 | tf_op jit(solution)/shard_map/cond/branch_0_fun/ppermute | solution.py:38
  24.5 1.6 %collective-permute-start = (bf16[128,1024]{1,0:T(8,128)(2,1)S(1)}, bf16[128,1024]{1,0:T(8,128)(2,1)S(1)}, u32[]{:S(2)}, u32[]{:S(2)}) collective-permute-start(bf16[128,1024]{1,0:T(8,128)(2,1)S(1)} %bitcast.29), channel_id=1, source_target_pairs={{7,0},{0,1},{1,2},{2,3},{3,4},{4,5},{5,6},{6,7},{15,8},{8,9},{9,10... | collective-permute-start | bytes 786440 | tf_op jit(solution)/shard_map/cond/branch_0_fun/ppermute | solution.py:46
  26.2 1.1 collective-permute-start.1
  27.4 2.2 %collective-permute-start.9 = (bf16[32,1024]{1,0:T(8,128)(2,1)S(1)}, bf16[32,1024]{1,0:T(8,128)(2,1)S(1)}, u32[]{:S(2)}, u32[]{:S(2)}) collective-permute-start(bf16[32,1024]{1,0:T(8,128)(2,1)S(1)} %copy-done.6), channel_id=1, source_target_pairs={{0,4},{1,5},{2,6},{3,7},{4,0},{5,1},{6,2},{7,3},{8,12},{9,13},{10,... | collective-permute-start | bytes 196616 | tf_op jit(solution)/shard_map/cond/branch_0_fun/ppermute | solution.py:38
  30.2 6.6 %collective-permute-done.9 = bf16[32,1024]{1,0:T(8,128)(2,1)S(1)} collective-permute-done((bf16[32,1024]{1,0:T(8,128)(2,1)S(1)}, bf16[32,1024]{1,0:T(8,128)(2,1)S(1)}, u32[]{:S(2)}, u32[]{:S(2)}) %collective-permute-start.9) | collective-permute-done | bytes 65568 | tf_op jit(solution)/shard_map/cond/branch_0_fun/ppermute | solution.py:38
  36.8 6.7 %collective-permute-start.10 = (bf16[64,1024]{1,0:T(8,128)(2,1)S(1)}, bf16[64,1024]{1,0:T(8,128)(2,1)S(1)}, u32[]{:S(2)}, u32[]{:S(2)}) collective-permute-start(bf16[64,1024]{1,0:T(8,128)(2,1)S(1)} %pad_maximum_fusion.1), channel_id=1, source_target_pairs={{0,1},{1,0},{2,3},{3,2},{4,5},{5,4},{6,7},{7,6},{8,10},{9,11},{10,... | collective-permute-start | bytes 393224 | tf_op jit(solution)/shard_map/cond/branch_0_fun/ppermute | solution.py:38
  43.5 1.3 %fusion.5 = s32[256]{0:T(256)S(1)} fusion(pred[]{:T(512)S(6)} %eq.37, s32[]{:T(128)} %bitcast.3, s32[]{:T(128)} %bitcast.2), kind=kLoop, calls=%fused_computation.36 | loop fusion | flops 4608 | bytes 1033 | tf_op jit(solution)/shard_map/cond/branch_0_fun/add | solution.py:256
  45.4 1.1 collective-permute-done.10
  46.5 3.2 %collective-permute-start.11 = (bf16[128,1024]{1,0:T(8,128)(2,1)S(1)}, bf16[128,1024]{1,0:T(8,128)(2,1)S(1)}, u32[]{:S(2)}, u32[]{:S(2)}) collective-permute-start(bf16[128,1024]{1,0:T(8,128)(2,1)S(1)} %constant_dynamic-update-slice_fusion.3.w0), channel_id=1, source_target_pairs={{0,2},{1,3},{2,0},{3,1},{4,6},{5,7},{6,4},{7,5},{8,9},{9,8},{10,11... | collective-permute-start | bytes 786440 | tf_op jit(solution)/shard_map/cond/branch_0_fun/ppermute | solution.py:38
  50.8 2.1 %collective-permute-start.8 = (bf16[128,1024]{1,0:T(8,128)(2,1)S(1)}, bf16[128,1024]{1,0:T(8,128)(2,1)S(1)}, u32[]{:S(2)}, u32[]{:S(2)}) collective-permute-start(bf16[128,1024]{1,0:T(8,128)(2,1)S(1)} %bitcast.30), channel_id=1, source_target_pairs={{7,0},{0,1},{1,2},{2,3},{3,4},{4,5},{5,6},{6,7},{15,8},{8,9},{9,10... | collective-permute-start | bytes 786440 | tf_op jit(solution)/shard_map/cond/branch_0_fun/ppermute | solution.py:46
  54.3 1.7 %norm.2 = (bf16[256,1024]{1,0:T(8,128)(2,1)S(1)}, bf16[256,1024]{1,0:T(8,128)(2,1)S(1)}, bf16[1024,256]{1,0:T(8,128)(2,1)S(1)}, f32[256,1]{1,0:T(8,128)S(1)}, f32[256,1]{1,0:T(8,128)S(1)}) custom-call(s32[2]{0:T(128)S(1)} %copy-done.8, s32[16]{0:T(128)S(1)} %pad_add_fusion.table.place_at.order, bf16[256,1024]{1,0:T(8,128)(2,1)} %bitcast.18, ...), custom_call_target="tpu_custom_call" | custom-call | flops 5242880 | bytes 2621440 | tf_op jit(solution)/shard_map/cond/branch_0_fun/norm/pallas_call | solution.py:265
  56.0 3.9 %fwd.2 = (bf16[1024,1536]{1,0:T(8,128)(2,1)S(1)}, bf16[256,1536]{1,0:T(8,128)(2,1)S(1)}, f32[8,256,256]{2,1,0:T(8,128)S(1)}, bf16[256,512]{1,0:T(8,128)(2,1)S(1)}, bf16[512,256]{1,0:T(8,128)(2,1)S(1)}) custom-call(s32[16]{0:T(128)S(1)} %pad_add_fusion.table.place_at.order, s32[16]{0:T(128)S(1)} %pad_add_fusion.table.place_at.order, ...), custom_call_target="tpu_custom_call" | custom-call | flops 2415919104 | bytes 10485760 | tf_op jit(solution)/shard_map/cond/branch_0_fun/fwd/pallas_call | solution.py:274
  59.9 1.0 collective-permute-done.8.halo
  60.9 1.0 term_out.2
  62.0 5.2 %bwd.2 = (bf16[512,1024]{1,0:T(8,128)(2,1)S(1)}, bf16[256,1536]{1,0:T(8,128)(2,1)S(1)}, f32[512,1536]{1,0:T(8,128)S(1)}, bf16[512,1536]{1,0:T(8,128)(2,1)S(1)}) custom-call(s32[16]{0:T(128)S(1)} %pad_add_fusion.table.place_at.order, bf16[256,1024]{1,0:T(8,128)(2,1)S(1)} %get-tuple-element.42.cot, bf16[256,1536]{1,0:T(8,128)(2,1)S(1)} %get-tuple-element.43.packed, ...), custom_call_target="tpu_custom_call" | custom-call | flops 3221225472 | bytes 12582912 | tf_op jit(solution)/shard_map/cond/branch_0_fun/bwd/pallas_call | solution.py:293
  67.7 2.9 %collective-permute-done.15 = bf16[512,1536]{1,0:T(8,128)(2,1)S(1)} collective-permute-done((bf16[512,1536]{1,0:T(8,128)(2,1)S(1)}, bf16[512,1536]{1,0:T(8,128)(2,1)S(1)}, u32[]{:S(2)}, u32[]{:S(2)}) %collective-permute-start.15) | collective-permute-done | bytes 1572896 | tf_op jit(solution)/shard_map/cond/branch_0_fun/ppermute | solution.py:42
  71.1 1.1 collective-permute-start.16
  72.4 1.1 collective-permute-start.20
  73.5 4.3 %collective-permute-start.7 = (bf16[128,512]{1,0:T(8,128)(2,1)S(1)}, bf16[128,512]{1,0:T(8,128)(2,1)S(1)}, u32[]{:S(2)}, u32[]{:S(2)}) collective-permute-start(bf16[128,512]{1,0:T(8,128)(2,1)S(1)} %slice.108), channel_id=1, source_target_pairs={{1,0},{2,1},{3,2},{4,3},{5,4},{6,5},{7,6},{0,7},{9,8},{10,9},{11,1... | collective-permute-start | bytes 393224 | tf_op jit(solution)/shard_map/cond/branch_0_fun/ppermute | solution.py:46
  78.5 1.3 %grad.2 = bf16[256,1024]{1,0:T(8,128)(2,1)S(1)} custom-call(bf16[256,1024]{1,0:T(8,128)(2,1)S(1)} %get-tuple-element.48.xw, f32[256,1]{1,0:T(8,128)S(1)} %get-tuple-element.49.mean, f32[256,1]{1,0:T(8,128)S(1)} %get-tuple-element.50.inv, bf16[256,1536]{1,0:T(8,128)(2,1)S(1)} %get-tuple-element.51.gp, bf16[1024,1536]{1,0:T(8,128)(2,1)S(1)} %get-tuple-element.52.full, ...), custom_call_target="tpu_custom_call" | custom-call | flops 805306368 | bytes 6291456 | tf_op jit(solution)/shard_map/cond/branch_0_fun/grad/pallas_call | solution.py:303
  79.8 1.5 %collective-permute-start.14 = (bf16[128,1024]{1,0:T(8,128)(2,1)S(1)}, bf16[128,1024]{1,0:T(8,128)(2,1)S(1)}, u32[]{:S(2)}, u32[]{:S(2)}) collective-permute-start(bf16[128,1024]{1,0:T(8,128)(2,1)S(1)} %slice.149), channel_id=1, source_target_pairs={{1,0},{2,1},{3,2},{4,3},{5,4},{6,5},{7,6},{0,7},{9,8},{10,9},{11,1... | collective-permute-start | bytes 786440 | tf_op jit(solution)/shard_map/cond/branch_0_fun/ppermute | solution.py:46
  81.3 8.9 %collective-permute-done.7.back = bf16[128,512]{1,0:T(8,128)(2,1)S(1)} collective-permute-done((bf16[128,512]{1,0:T(8,128)(2,1)S(1)}, bf16[128,512]{1,0:T(8,128)(2,1)S(1)}, u32[]{:S(2)}, u32[]{:S(2)}) %collective-permute-start.7) | collective-permute-done | bytes 131104 | tf_op jit(solution)/shard_map/cond/branch_0_fun/ppermute | solution.py:46
  90.1 1.8 %output.2 = bf16[256,1024]{1,0:T(8,128)(2,1)} custom-call(s32[2]{0:T(128)S(1)} %copy-done.8, bf16[256,1024]{1,0:T(8,128)(2,1)S(1)} %bitcast.19, bf16[256,512]{1,0:T(8,128)(2,1)S(1)} %get-tuple-element.39.ctx, bf16[128,512]{1,0:T(8,128)(2,1)S(1)} %collective-permute-done.7.back, bf16[512,1024]{1,0:T(8,128)(2,1)S(1)} %get-tuple-element.47.full), custom_call_target="tpu_custom_call" | custom-call | flops 268435456 | bytes 3145728 | tf_op jit(solution)/shard_map/cond/branch_0_fun/output/pallas_call | solution.py:312
  92.0 3.1 %collective-permute-start.21 = (bf16[64,1024]{1,0:T(8,128)(2,1)S(1)}, bf16[64,1024]{1,0:T(8,128)(2,1)S(1)}, u32[]{:S(2)}, u32[]{:S(2)}) collective-permute-start(bf16[64,1024]{1,0:T(8,128)(2,1)S(1)} %slice.204), channel_id=1, source_target_pairs={{0,1},{1,0},{2,3},{3,2},{4,5},{5,4},{6,7},{7,6},{8,10},{9,11},{10,... | collective-permute-start | bytes 393224 | tf_op jit(solution)/shard_map/cond/branch_0_fun/ppermute | solution.py:38
  96.4 1.6 %collective-permute-done.21 = bf16[64,1024]{1,0:T(8,128)(2,1)S(1)} collective-permute-done((bf16[64,1024]{1,0:T(8,128)(2,1)S(1)}, bf16[64,1024]{1,0:T(8,128)(2,1)S(1)}, u32[]{:S(2)}, u32[]{:S(2)}) %collective-permute-start.21) | collective-permute-done | bytes 131104 | tf_op jit(solution)/shard_map/cond/branch_0_fun/ppermute | solution.py:38
  98.1 4.6 %collective-permute-start.22 = (bf16[32,1024]{1,0:T(8,128)(2,1)S(1)}, bf16[32,1024]{1,0:T(8,128)(2,1)S(1)}, u32[]{:S(2)}, u32[]{:S(2)}) collective-permute-start(bf16[32,1024]{1,0:T(8,128)(2,1)S(1)} %slice.205), channel_id=1, source_target_pairs={{0,4},{1,5},{2,6},{3,7},{4,0},{5,1},{6,2},{7,3},{8,12},{9,13},{10,... | collective-permute-start | bytes 196616 | tf_op jit(solution)/shard_map/cond/branch_0_fun/ppermute | solution.py:38
  103.3 4.6 %collective-permute-start.18 = (bf16[64,1536]{1,0:T(8,128)(2,1)S(1)}, bf16[64,1536]{1,0:T(8,128)(2,1)S(1)}, u32[]{:S(2)}, u32[]{:S(2)}) collective-permute-start(bf16[64,1536]{1,0:T(8,128)(2,1)S(1)} %slice.203), channel_id=1, source_target_pairs={{0,4},{1,5},{2,6},{3,7},{4,0},{5,1},{6,2},{7,3},{8,12},{9,13},{10,... | collective-permute-start | bytes 589832 | tf_op jit(solution)/shard_map/cond/branch_0_fun/ppermute | solution.py:38
  108.6 9.1 %collective-permute-done.18 = bf16[64,1536]{1,0:T(8,128)(2,1)S(1)} collective-permute-done((bf16[64,1536]{1,0:T(8,128)(2,1)S(1)}, bf16[64,1536]{1,0:T(8,128)(2,1)S(1)}, u32[]{:S(2)}, u32[]{:S(2)}) %collective-permute-start.18) | collective-permute-done | bytes 196640 | tf_op jit(solution)/shard_map/cond/branch_0_fun/ppermute | solution.py:38
  (76 shorter events, 12.2 us)
Async XLA Ops:
  1.3 23.2 %copy-start = (bf16[1,16,16,1024]{3,2,1,0:T(8,128)(2,1)S(1)}, bf16[1,16,16,1024]{3,2,1,0:T(8,128)(2,1)}, u32[]{:S(2)}) copy-start(bf16[1,16,16,1024]{3,2,1,0:T(8,128)(2,1)} %get-tuple-element.33) | copy-start | bytes 1572868 | tf_op jit(solution)/shard_map/cond
  1.3 24.8 %copy-start.10 = (s32[1,16,16]{2,1,0:T(8,128)S(1)}, s32[1,16,16]{2,1,0:T(8,128)}, u32[]{:S(2)}) copy-start(s32[1,16,16]{2,1,0:T(8,128)} %get-tuple-element.37) | copy-start | bytes 3076 | tf_op jit(solution)/shard_map/cond
  1.3 26.0 %copy-start.6 = (bf16[32,1024]{1,0:T(8,128)(2,1)S(1)}, bf16[32,1024]{1,0:T(8,128)(2,1)}, u32[]{:S(2)}) copy-start(bf16[32,1024]{1,0:T(8,128)(2,1)} %get-tuple-element.46) | copy-start | bytes 196612 | tf_op jit(solution)/shard_map/cond
  1.3 28.2 %copy-start.12 = (s32[8]{0:T(128)S(1)}, s32[8]{0:T(128)}, u32[]{:S(2)}) copy-start(s32[8]{0:T(128)} %get-tuple-element.34) | copy-start | bytes 100 | tf_op jit(solution)/shard_map/cond
  1.3 28.2 %copy-start.14 = (s32[8]{0:T(128)S(1)}, s32[8]{0:T(128)}, u32[]{:S(2)}) copy-start(s32[8]{0:T(128)} %get-tuple-element.35) | copy-start | bytes 100 | tf_op jit(solution)/shard_map/cond
  1.4 28.3 %copy-start.8 = (s32[2]{0:T(128)S(1)}, s32[2]{0:T(128)}, u32[]{:S(2)}) copy-start(s32[2]{0:T(128)} %get-tuple-element.32.scal) | copy-start | bytes 28 | tf_op jit(solution)/shard_map/cond
  1.4 13.4 %collective-permute-start.2 = (bf16[64,1536]{1,0:T(8,128)(2,1)}, bf16[64,1536]{1,0:T(8,128)(2,1)S(1)}, u32[]{:S(2)}, u32[]{:S(2)}) collective-permute-start(bf16[64,1536]{1,0:T(8,128)(2,1)} %get-tuple-element.38), channel_id=1, source_target_pairs={{0,4},{1,5},{2,6},{3,7},{4,0},{5,1},{6,2},{7,3},{8,12},{9,13},{10,... | collective-permute-start | bytes 589832 | tf_op jit(solution)/shard_map/cond/branch_0_fun/ppermute | solution.py:38
  15.7 7.8 %collective-permute-start.3 = (bf16[128,1536]{1,0:T(8,128)(2,1)S(1)}, bf16[128,1536]{1,0:T(8,128)(2,1)S(1)}, u32[]{:S(2)}, u32[]{:S(2)}) collective-permute-start(bf16[128,1536]{1,0:T(8,128)(2,1)S(1)} %pad_maximum_fusion), channel_id=1, source_target_pairs={{0,1},{1,0},{2,3},{3,2},{4,5},{5,4},{6,7},{7,6},{8,10},{9,11},{10,... | collective-permute-start | bytes 1179656 | tf_op jit(solution)/shard_map/cond/branch_0_fun/ppermute | solution.py:38
  23.6 21.3 %collective-permute-start.4 = (bf16[256,1536]{1,0:T(8,128)(2,1)S(1)}, bf16[256,1536]{1,0:T(8,128)(2,1)S(1)}, u32[]{:S(2)}, u32[]{:S(2)}) collective-permute-start(bf16[256,1536]{1,0:T(8,128)(2,1)S(1)} %constant_dynamic-update-slice_fusion.w0), channel_id=1, source_target_pairs={{0,2},{1,3},{2,0},{3,1},{4,6},{5,7},{6,4},{7,5},{8,9},{9,8},{10,11... | collective-permute-start | bytes 2359304 | tf_op jit(solution)/shard_map/cond/branch_0_fun/ppermute | solution.py:38
  24.5 29.1 %collective-permute-start = (bf16[128,1024]{1,0:T(8,128)(2,1)S(1)}, bf16[128,1024]{1,0:T(8,128)(2,1)S(1)}, u32[]{:S(2)}, u32[]{:S(2)}) collective-permute-start(bf16[128,1024]{1,0:T(8,128)(2,1)S(1)} %bitcast.29), channel_id=1, source_target_pairs={{7,0},{0,1},{1,2},{2,3},{3,4},{4,5},{5,6},{6,7},{15,8},{8,9},{9,10... | collective-permute-start | bytes 786440 | tf_op jit(solution)/shard_map/cond/branch_0_fun/ppermute | solution.py:46
  26.2 24.6 %collective-permute-start.1 = (bf16[128,1]{0,1:T(2,128)(2,1)S(1)}, bf16[128,1]{0,1:T(2,128)(2,1)S(1)}, u32[]{:S(2)}, u32[]{:S(2)}) collective-permute-start(bf16[128,1]{0,1:T(2,128)(2,1)S(1)} %slice.107), channel_id=1, source_target_pairs={{7,0},{0,1},{1,2},{2,3},{3,4},{4,5},{5,6},{6,7},{15,8},{8,9},{9,10... | collective-permute-start | bytes 776 | tf_op jit(solution)/shard_map/cond/branch_0_fun/ppermute | solution.py:46
  27.4 9.5 %collective-permute-start.9 = (bf16[32,1024]{1,0:T(8,128)(2,1)S(1)}, bf16[32,1024]{1,0:T(8,128)(2,1)S(1)}, u32[]{:S(2)}, u32[]{:S(2)}) collective-permute-start(bf16[32,1024]{1,0:T(8,128)(2,1)S(1)} %copy-done.6), channel_id=1, source_target_pairs={{0,4},{1,5},{2,6},{3,7},{4,0},{5,1},{6,2},{7,3},{8,12},{9,13},{10,... | collective-permute-start | bytes 196616 | tf_op jit(solution)/shard_map/cond/branch_0_fun/ppermute | solution.py:38
  36.8 9.6 %collective-permute-start.10 = (bf16[64,1024]{1,0:T(8,128)(2,1)S(1)}, bf16[64,1024]{1,0:T(8,128)(2,1)S(1)}, u32[]{:S(2)}, u32[]{:S(2)}) collective-permute-start(bf16[64,1024]{1,0:T(8,128)(2,1)S(1)} %pad_maximum_fusion.1), channel_id=1, source_target_pairs={{0,1},{1,0},{2,3},{3,2},{4,5},{5,4},{6,7},{7,6},{8,10},{9,11},{10,... | collective-permute-start | bytes 393224 | tf_op jit(solution)/shard_map/cond/branch_0_fun/ppermute | solution.py:38
  44.8 11.2 %collective-permute-start.5 = (bf16[256,1536]{1,0:T(8,128)(2,1)S(1)}, bf16[256,1536]{1,0:T(8,128)(2,1)S(1)}, u32[]{:S(2)}, u32[]{:S(2)}) collective-permute-start(bf16[256,1536]{1,0:T(8,128)(2,1)S(1)} %constant_dynamic-update-slice_fusion.w0), channel_id=1, source_target_pairs={{0,8},{8,0},{1,9},{9,1},{2,10},{10,2},{3,11},{11,3},{4,12},{12,4},... | collective-permute-start | bytes 2359304 | tf_op jit(solution)/shard_map/cond/branch_0_fun/ppermute | solution.py:42
  44.9 11.1 %collective-permute-start.6 = (bf16[256,1536]{1,0:T(8,128)(2,1)S(1)}, bf16[256,1536]{1,0:T(8,128)(2,1)}, u32[]{:S(2)}, u32[]{:S(2)}) collective-permute-start(bf16[256,1536]{1,0:T(8,128)(2,1)S(1)} %collective-permute-done.4.w1), channel_id=1, source_target_pairs={{0,8},{8,0},{1,9},{9,1},{2,10},{10,2},{3,11},{11,3},{4,12},{12,4},... | collective-permute-start | bytes 2359304 | tf_op jit(solution)/shard_map/cond/branch_0_fun/ppermute | solution.py:42
  46.5 7.6 %collective-permute-start.11 = (bf16[128,1024]{1,0:T(8,128)(2,1)S(1)}, bf16[128,1024]{1,0:T(8,128)(2,1)S(1)}, u32[]{:S(2)}, u32[]{:S(2)}) collective-permute-start(bf16[128,1024]{1,0:T(8,128)(2,1)S(1)} %constant_dynamic-update-slice_fusion.3.w0), channel_id=1, source_target_pairs={{0,2},{1,3},{2,0},{3,1},{4,6},{5,7},{6,4},{7,5},{8,9},{9,8},{10,11... | collective-permute-start | bytes 786440 | tf_op jit(solution)/shard_map/cond/branch_0_fun/ppermute | solution.py:38
  50.8 10.1 %collective-permute-start.8 = (bf16[128,1024]{1,0:T(8,128)(2,1)S(1)}, bf16[128,1024]{1,0:T(8,128)(2,1)S(1)}, u32[]{:S(2)}, u32[]{:S(2)}) collective-permute-start(bf16[128,1024]{1,0:T(8,128)(2,1)S(1)} %bitcast.30), channel_id=1, source_target_pairs={{7,0},{0,1},{1,2},{2,3},{3,4},{4,5},{5,6},{6,7},{15,8},{8,9},{9,10... | collective-permute-start | bytes 786440 | tf_op jit(solution)/shard_map/cond/branch_0_fun/ppermute | solution.py:46
  53.6 8.3 %collective-permute-start.12 = (bf16[128,1024]{1,0:T(8,128)(2,1)S(1)}, bf16[128,1024]{1,0:T(8,128)(2,1)S(1)}, u32[]{:S(2)}, u32[]{:S(2)}) collective-permute-start(bf16[128,1024]{1,0:T(8,128)(2,1)S(1)} %constant_dynamic-update-slice_fusion.3.w0), channel_id=1, source_target_pairs={{0,8},{8,0},{1,9},{9,1},{2,10},{10,2},{3,11},{11,3},{4,12},{12,4},... | collective-permute-start | bytes 786440 | tf_op jit(solution)/shard_map/cond/branch_0_fun/ppermute | solution.py:42
  54.0 7.9 %collective-permute-start.13 = (bf16[128,1024]{1,0:T(8,128)(2,1)S(1)}, bf16[128,1024]{1,0:T(8,128)(2,1)S(1)}, u32[]{:S(2)}, u32[]{:S(2)}) collective-permute-start(bf16[128,1024]{1,0:T(8,128)(2,1)S(1)} %collective-permute-done.11.w1), channel_id=1, source_target_pairs={{0,8},{8,0},{1,9},{9,1},{2,10},{10,2},{3,11},{11,3},{4,12},{12,4},... | collective-permute-start | bytes 786440 | tf_op jit(solution)/shard_map/cond/branch_0_fun/ppermute | solution.py:42
  56.0 4.9 %copy-start.4 = (bf16[1,16,16,1024]{3,2,1,0:T(8,128)(2,1)S(1)}, bf16[1,16,16,1024]{3,2,1,0:T(8,128)(2,1)}, u32[]{:S(2)}) copy-start(bf16[1,16,16,1024]{3,2,1,0:T(8,128)(2,1)} %get-tuple-element.41) | copy-start | bytes 1572868 | tf_op jit(solution)/shard_map/cond
  67.1 3.5 %collective-permute-start.15 = (bf16[512,1536]{1,0:T(8,128)(2,1)S(1)}, bf16[512,1536]{1,0:T(8,128)(2,1)S(1)}, u32[]{:S(2)}, u32[]{:S(2)}) collective-permute-start(bf16[512,1536]{1,0:T(8,128)(2,1)S(1)} %get-tuple-element.54), channel_id=1, source_target_pairs={{0,8},{8,0},{1,9},{9,1},{2,10},{10,2},{3,11},{11,3},{4,12},{12,4},... | collective-permute-start | bytes 4718600 | tf_op jit(solution)/shard_map/cond/branch_0_fun/ppermute | solution.py:42
  67.2 5.0 %collective-permute-start.19 = (bf16[256,1024]{1,0:T(8,128)(2,1)S(1)}, bf16[256,1024]{1,0:T(8,128)(2,1)S(1)}, u32[]{:S(2)}, u32[]{:S(2)}) collective-permute-start(bf16[256,1024]{1,0:T(8,128)(2,1)S(1)} %get-tuple-element.56), channel_id=1, source_target_pairs={{0,8},{8,0},{1,9},{9,1},{2,10},{10,2},{3,11},{11,3},{4,12},{12,4},... | collective-permute-start | bytes 1572872 | tf_op jit(solution)/shard_map/cond/branch_0_fun/ppermute | solution.py:42
  71.1 24.0 %collective-permute-start.16 = (bf16[256,1536]{1,0:T(8,128)(2,1)S(1)}, bf16[256,1536]{1,0:T(8,128)(2,1)S(1)}, u32[]{:S(2)}, u32[]{:S(2)}) collective-permute-start(bf16[256,1536]{1,0:T(8,128)(2,1)S(1)} %slice.200), channel_id=1, source_target_pairs={{0,2},{1,3},{2,0},{3,1},{4,6},{5,7},{6,4},{7,5},{8,9},{9,8},{10,11... | collective-permute-start | bytes 2359304 | tf_op jit(solution)/shard_map/cond/branch_0_fun/ppermute | solution.py:38
  72.4 19.5 %collective-permute-start.20 = (bf16[128,1024]{1,0:T(8,128)(2,1)S(1)}, bf16[128,1024]{1,0:T(8,128)(2,1)S(1)}, u32[]{:S(2)}, u32[]{:S(2)}) collective-permute-start(bf16[128,1024]{1,0:T(8,128)(2,1)S(1)} %slice.202), channel_id=1, source_target_pairs={{0,2},{1,3},{2,0},{3,1},{4,6},{5,7},{6,4},{7,5},{8,9},{9,8},{10,11... | collective-permute-start | bytes 786440 | tf_op jit(solution)/shard_map/cond/branch_0_fun/ppermute | solution.py:38
  73.5 16.6 %collective-permute-start.7 = (bf16[128,512]{1,0:T(8,128)(2,1)S(1)}, bf16[128,512]{1,0:T(8,128)(2,1)S(1)}, u32[]{:S(2)}, u32[]{:S(2)}) collective-permute-start(bf16[128,512]{1,0:T(8,128)(2,1)S(1)} %slice.108), channel_id=1, source_target_pairs={{1,0},{2,1},{3,2},{4,3},{5,4},{6,5},{7,6},{0,7},{9,8},{10,9},{11,1... | collective-permute-start | bytes 393224 | tf_op jit(solution)/shard_map/cond/branch_0_fun/ppermute | solution.py:46
  78.5 11.7 %copy-start.1 = (bf16[1,16,16,1024]{3,2,1,0:T(8,128)(2,1)S(1)}, bf16[1,16,16,1024]{3,2,1,0:T(8,128)(2,1)}, u32[]{:S(2)}) copy-start(bf16[1,16,16,1024]{3,2,1,0:T(8,128)(2,1)} %get-tuple-element.33) | copy-start | bytes 1572868 | tf_op jit(solution)/shard_map/cond
  79.8 15.7 %collective-permute-start.14 = (bf16[128,1024]{1,0:T(8,128)(2,1)S(1)}, bf16[128,1024]{1,0:T(8,128)(2,1)S(1)}, u32[]{:S(2)}, u32[]{:S(2)}) collective-permute-start(bf16[128,1024]{1,0:T(8,128)(2,1)S(1)} %slice.149), channel_id=1, source_target_pairs={{1,0},{2,1},{3,2},{4,3},{5,4},{6,5},{7,6},{0,7},{9,8},{10,9},{11,1... | collective-permute-start | bytes 786440 | tf_op jit(solution)/shard_map/cond/branch_0_fun/ppermute | solution.py:46
  92.0 6.1 %collective-permute-start.21 = (bf16[64,1024]{1,0:T(8,128)(2,1)S(1)}, bf16[64,1024]{1,0:T(8,128)(2,1)S(1)}, u32[]{:S(2)}, u32[]{:S(2)}) collective-permute-start(bf16[64,1024]{1,0:T(8,128)(2,1)S(1)} %slice.204), channel_id=1, source_target_pairs={{0,1},{1,0},{2,3},{3,2},{4,5},{5,4},{6,7},{7,6},{8,10},{9,11},{10,... | collective-permute-start | bytes 393224 | tf_op jit(solution)/shard_map/cond/branch_0_fun/ppermute | solution.py:38
  95.4 7.8 %collective-permute-start.17 = (bf16[128,1536]{1,0:T(8,128)(2,1)S(1)}, bf16[128,1536]{1,0:T(8,128)(2,1)S(1)}, u32[]{:S(2)}, u32[]{:S(2)}) collective-permute-start(bf16[128,1536]{1,0:T(8,128)(2,1)S(1)} %slice.201), channel_id=1, source_target_pairs={{0,1},{1,0},{2,3},{3,2},{4,5},{5,4},{6,7},{7,6},{8,10},{9,11},{10,... | collective-permute-start | bytes 1179656 | tf_op jit(solution)/shard_map/cond/branch_0_fun/ppermute | solution.py:38
  98.1 9.8 %collective-permute-start.22 = (bf16[32,1024]{1,0:T(8,128)(2,1)S(1)}, bf16[32,1024]{1,0:T(8,128)(2,1)S(1)}, u32[]{:S(2)}, u32[]{:S(2)}) collective-permute-start(bf16[32,1024]{1,0:T(8,128)(2,1)S(1)} %slice.205), channel_id=1, source_target_pairs={{0,4},{1,5},{2,6},{3,7},{4,0},{5,1},{6,2},{7,3},{8,12},{9,13},{10,... | collective-permute-start | bytes 196616 | tf_op jit(solution)/shard_map/cond/branch_0_fun/ppermute | solution.py:38
  103.3 14.4 %collective-permute-start.18 = (bf16[64,1536]{1,0:T(8,128)(2,1)S(1)}, bf16[64,1536]{1,0:T(8,128)(2,1)S(1)}, u32[]{:S(2)}, u32[]{:S(2)}) collective-permute-start(bf16[64,1536]{1,0:T(8,128)(2,1)S(1)} %slice.203), channel_id=1, source_target_pairs={{0,4},{1,5},{2,6},{3,7},{4,0},{5,1},{6,2},{7,3},{8,12},{9,13},{10,... | collective-permute-start | bytes 589832 | tf_op jit(solution)/shard_map/cond/branch_0_fun/ppermute | solution.py:38

commit v3 on v2

--- a/solution.py
+++ b/solution.py
@@ -146,21 +146,17 @@
     keep[...] = dot(ctx_ordered[pl.ds(0, n), :], cot[...])
 
 
-def backward_kernel(place_at, cot, packed, attn, ordered, w0, w1, w2, w3, full, gp, keep, send, gctx, *, blocks):
-    size = full.shape[0] // blocks
-    quarter = blocks // 4
-    for i, w in enumerate((w0, w1, w2, w3)):
-        place(full, w, place_at, i * quarter, quarter, size)
-    hidden = full.shape[0]
-    cells = cot.shape[0]
-    gctx[...] = dot(cot[...], full[...], 1, 1).astype(BF16)
+def half_backward(packed, attn, gctx, gp, first_pair, pairs):
+    cells = packed.shape[0]
+    hidden = packed.shape[1] // 3
+    width = pairs * PAIR
     first = lax.broadcasted_iota(jnp.int32, (cells, PAIR), 1) < HD
-    for p in range(HEADS // 2):
-        lanes = pl.ds(p * PAIR, PAIR)
-        q = packed[:, lanes]
+    for i in range(pairs):
+        p = first_pair + i
+        q = packed[:, pl.ds(p * PAIR, PAIR)]
         k = packed[:, pl.ds(hidden + p * PAIR, PAIR)]
         v = packed[:, pl.ds(2 * hidden + p * PAIR, PAIR)]
-        g = gctx[:, lanes]
+        g = gctx[:, pl.ds(p * PAIR, PAIR)]
         gf = g.astype(F32)
         gq, gk, gv = [], [], []
         for side in range(2):
@@ -172,15 +168,36 @@
             gq.append(dot(gs, k))
             gk.append(dot(gs, q, 0, 0))
             gv.append(dot(a.astype(BF16), g, 0, 0))
-        gp[:, lanes] = jnp.where(first, gq[0], gq[1]).astype(BF16)
-        gp[:, pl.ds(hidden + p * PAIR, PAIR)] = jnp.where(first, gk[0], gk[1]).astype(BF16)
-        gp[:, pl.ds(2 * hidden + p * PAIR, PAIR)] = jnp.where(first, gv[0], gv[1]).astype(BF16)
+        for t, two in enumerate((gq, gk, gv)):
+            gp[:, pl.ds(t * width + i * PAIR, PAIR)] = jnp.where(first, two[0], two[1]).astype(BF16)
+
+
+def term_of(ordered, gp, keep, send):
     n = keep.shape[0]
     send[...] = dot(ordered[pl.ds(n, n), :], gp[...]).astype(BF16)
     keep[...] = dot(ordered[pl.ds(0, n), :], gp[...])
 
 
-def grad_kernel(xw, mean, inv, gp, full, cot, grad):
+def backward_a_kernel(place_at, cot, packed, attn, ordered, w0, w1, w2, w3, full, gctx, gp, keep, send, *, blocks):
+    size = full.shape[0] // blocks
+    quarter = blocks // 4
+    for i, w in enumerate((w0, w1, w2, w3)):
+        place(full, w, place_at, i * quarter, quarter, size)
+    gctx[...] = dot(cot[...], full[...], 1, 1).astype(BF16)
+    half_backward(packed, attn, gctx, gp, 0, HEADS // 4)
+    term_of(ordered, gp, keep, send)
+
+
+def backward_b_kernel(packed, attn, gctx, ordered, gp, keep, send):
+    half_backward(packed, attn, gctx, gp, HEADS // 4, HEADS // 4)
+    term_of(ordered, gp, keep, send)
+
+
+def grad_kernel(xw, mean, inv, gp_a, gp_b, full, cot, grad, gp):
+    width = gp.shape[1] // 6
+    for t in range(3):
+        gp[:, pl.ds(2 * t * width, width)] = gp_a[:, pl.ds(t * width, width)]
+        gp[:, pl.ds((2 * t + 1) * width, width)] = gp_b[:, pl.ds(t * width, width)]
     gn = dot(gp[...], full[...], 1, 1)
     normed = (xw[...].astype(F32) - mean[...]) * inv[...]
     m1 = jnp.mean(gn, axis=-1, keepdims=True)
@@ -199,23 +216,41 @@
     out[...] = (own[...].astype(F32) + dot(mixed[...], full[...])).astype(BF16)
 
 
-def gather_parts(shard, rows):
+def after(value, *done):
+    return lax.optimization_barrier((value, *done))[0]
+
+
+def gather_parts(shard, rows, waits):
     stages = len(stage_masks(rows)[0])
-    held = shard
+    held, arrived = shard, []
     for stage in range(stages - 1):
-        held = jnp.concatenate([held, exchange(held, rows, stage)], axis=0)
-    last = exchange(held, rows, stages - 1)
-    return held, last, swap_cores(held), swap_cores(last)
-
-
-def scatter_parts(keep, send, rows):
+        got = exchange(after(held, *waits[stage]) if waits[stage] else held, rows, stage)
+        arrived.append(got)
+        held = jnp.concatenate([held, got], axis=0)
+    last = exchange(after(held, *waits[-1]) if waits[-1] else held, rows, stages - 1)
+    arrived.append(last)
+    return (held, last, swap_cores(held), swap_cores(last)), arrived
+
+
+def scatter_from(keep, arrived, rows):
     stages = len(stage_masks(rows)[0])
-    keep = keep + swap_cores(send).astype(F32)
+    keep = keep + arrived.astype(F32)
+    first, seen = keep, []
     for stage in range(stages - 1, -1, -1):
         half = keep.shape[0] // 2
         arrived = exchange(keep[half:].astype(BF16), rows, stage)
-        keep = keep[:half] + arrived.astype(F32)
-    return keep
+        seen.append(arrived)
+        if stage:
+            keep = keep[:half] + arrived.astype(F32)
+    return keep[: keep.shape[0] // 2], arrived, first, seen
+
+
+def finish_kernel(keep_a, last_a, keep_b, last_b, out):
+    fine = keep_a.shape[1] // 3
+    for i, (keep, last) in enumerate(((keep_a, last_a), (keep_b, last_b))):
+        for t in range(3):
+            cols = pl.ds(t * fine, fine)
+            out[:, pl.ds((2 * t + i) * fine, fine)] = keep[:, cols] + last[:, cols].astype(F32)
 
 
 def branch(tokens, cell_mask, shifts, projection_in, projection_out, cotangent, *, forward):
@@ -243,9 +278,13 @@
     own_mask = cell_mask.astype(BF16).reshape(cells, 1)
     halo = shifted(part(own), rows, distance)
     halo_mask = shifted(part(own_mask), rows, distance)
-    in_parts = gather_parts(projection_in, rows)
-    out_parts = gather_parts(projection_out, rows)
-    halo_cot = shifted(part(own_cot), rows, distance)
+    stages = len(stage_masks(rows)[0])
+    waits = [()] * stages
+    waits[1] = (halo, halo_mask)
+    in_parts, in_got = gather_parts(projection_in, rows, waits)
+    waits = [(in_got[t],) for t in range(stages)]
+    out_parts, out_got = gather_parts(projection_out, rows, waits)
+    halo_cot = shifted(after(part(own_cot), in_got[-1]), rows, distance)
 
     cell = jnp.arange(cells, dtype=jnp.int32)
     cell_row, cell_col = cell // cols, cell % cols
@@ -289,25 +328,47 @@
         moved=4 << 20,
         name="term_out",
     )(scal, ctx_ordered, own_cot, halo_cot)
-    grad_out = scatter_parts(keep_out, send_out, rows)
-    full_out, gp, keep_in, send_in = call(
-        functools.partial(backward_kernel, blocks=blocks),
-        [((hidden, dim), BF16), ((cells, 3 * hidden), BF16), ((dim // 2, 3 * hidden), F32), ((dim // 2, 3 * hidden), BF16)],
+    swapped_out = swap_cores(send_out)
+    quart = 3 * hidden // 2
+    half_outs = [((cells, quart), BF16), ((dim // 2, quart), F32), ((dim // 2, quart), BF16)]
+    full_out, gctx, gp_a, keep_a, send_a = call(
+        functools.partial(backward_a_kernel, blocks=blocks),
+        [((hidden, dim), BF16), ((cells, hidden), BF16)] + half_outs,
         [SM, VM, VM, VM, VM, VM, VM, VM, VM],
-        [pltpu.VMEM((cells, hidden), BF16)],
-        flops=8 * cells * dim * 3 * hidden,
-        moved=12 << 20,
-        name="bwd",
+        flops=4 * cells * dim * 3 * hidden,
+        moved=6 << 20,
+        name="bwd_a",
     )(table, cot, packed, attn, ordered, *out_parts)
-    grad_in = scatter_parts(keep_in, send_in, rows)
+    swapped_a = swap_cores(send_a)
+    gp_b, keep_b, send_b = call(
+        backward_b_kernel,
+        half_outs,
+        [VM, VM, VM, VM],
+        flops=4 * cells * dim * 3 * hidden,
+        moved=6 << 20,
+        name="bwd_b",
+    )(packed, attn, after(gctx, swapped_out), ordered)
+    swapped_b = swap_cores(send_b)
+    kept_out, last_out, _, _ = scatter_from(keep_out, swapped_out, rows)
+    grad_out = kept_out + last_out.astype(F32)
+    kept_a, last_a, first_a, seen_a = scatter_from(keep_a, swapped_a, rows)
+    kept_b, last_b, _, _ = scatter_from(keep_b, swapped_b, rows)
+    (grad_in,) = call(
+        finish_kernel,
+        [((dim // blocks, 3 * hidden), F32)],
+        [VM] * 4,
+        moved=1 << 20,
+        name="finish",
+    )(kept_a, last_a, kept_b, last_b)
     (grad_win,) = call(
         grad_kernel,
         [((cells, dim), BF16)],
-        [VM] * 6,
+        [VM] * 7,
+        [pltpu.VMEM((cells, 3 * hidden), BF16)],
         flops=2 * cells * dim * 3 * hidden,
         moved=6 << 20,
         name="grad",
-    )(xw, mean, inv, gp, full_in, cot)
+    )(xw, mean, inv, gp_a, after(gp_b, back_ctx, first_a), full_in, cot)
     back_grad = shifted(part(grad_win), rows, -distance)
     (output,) = call(
         functools.partial(output_kernel, **shape_kw),
@@ -317,7 +378,7 @@
         flops=2 * cells * dim * hidden,
         moved=3 << 20,
         name="output",
-    )(scal, own, ctx, back_ctx, full_out)
+    )(scal, own, ctx, after(back_ctx, seen_a[0]), full_out)
     own_grad = jnp.where(from_other[:, None], jnp.pad(back_grad, pad), grad_win)
     shape = tokens.shape
     return (output.reshape(shape), own_grad.reshape(shape), grad_in, grad_out)

time: 119 us -> 106 us (0.89)
  waiting for transfers between devices: 46.8 us -> 26 us
  starting transfers between devices: 45.1 us -> 52.9 us
    ppermute x12 -> x15, waiting for transfers between devices: 33.9 us -> 23.6 us  [exchange(): return lax.ppermute(block, ('fsdp', 'rows'), pairs)]
    ppermute x12 -> x15, starting transfers between devices: 33.2 us -> 42.5 us  [exchange(): return lax.ppermute(block, ('fsdp', 'rows'), pairs)]
    ppermute x5, waiting for transfers between devices: 9.92 us -> 0.89 us  [shifted(): lax.ppermute(block, 'rows', [((i - distance) % rows, i) for i in range(ro...]
    ppermute x6 -> x7, waiting for transfers between devices: 2.91 us -> 1.55 us  [swap_cores(): return lax.ppermute(block, 'fsdp', [(0, 1), (1, 0)])]
    pallas_call x2 -> x4, Pallas kernels: 6.43 us -> 7.64 us  [the longest x1 3.34 us: branch(): call(functools.partial(backward_a_kernel, blocks=blocks), [((hidden, dim)...]
    add x8 -> x10, other arithmetic: 2.45 us -> 1.43 us  [the longest x1 0.67 us: branch(): grad_out = kept_out + last_out.astype(F32)]
  transfers between devices with their start and end apart: 23 -> 27, of which waited for: 11 -> 12; matrix products, arithmetic and copies ran while one was open for 7% -> 9% of each run, Pallas kernels for 8% -> 13%
where the time goes in v3:
time: 106 us
  starting transfers between devices  52.9 us (50%)
  waiting for transfers between devices  26 us (25%)
  Pallas kernels  14.9 us (14%)
  other arithmetic  6.86 us (6%)
  local copies, waits for them, and re-layouts  3.08 us (3%)
  between operations  1.28 us (1%)
    ppermute x15, starting transfers between devices, exchange(): return lax.ppermute(block, ('fsdp', 'rows'), pairs)  42.5 us
    ppermute x15, waiting for transfers between devices, exchange(): return lax.ppermute(block, ('fsdp', 'rows'), pairs)  23.6 us
    ppermute x5, starting transfers between devices, shifted(): lax.ppermute(block, 'rows', [((i - distance) % rows, i) for i in range(ro...  9.59 us
    pallas_call x1, Pallas kernels, branch(): call(functools.partial(backward_a_kernel, blocks=blocks), [((hidden, dim)...  3.34 us
    pallas_call x1, Pallas kernels, branch(): call(functools.partial(forward_kernel, blocks=blocks), [((dim, 3 * hidden...  3.3 us
    pallas_call x1, Pallas kernels, branch(): call(backward_b_kernel, half_outs, [VM, VM, VM, VM], flops=4 * cells * di...  2.23 us
  transfers between devices with their start and end apart: 27, of which 12 were waited for; matrix products, arithmetic and copies ran while one was open for 9% of the time, Pallas kernels for 13%

profile of v3, /device:TPU:0, one launch (start us, length us, event | category | flops | bytes accessed | tf_op | source)
XLA Modules:
  0.0 105.8 jit_solution(5406459356470496695)
XLA Ops:
  1.3 104.5 %conditional.1 = (bf16[1,16,16,1024]{3,2,1,0:T(8,128)(2,1)}, bf16[1,16,16,1024]{3,2,1,0:T(8,128)(2,1)}, f32[64,1536]{1,0:T(8,128)}, f32[32,1024]{1,0:T(8,128)}) conditional(s32[]{:T(128)} %bitcast.16, (bf16[1,16,16,1024]{3,2,1,0:T(8,128)(2,1)}, s32[8]{0:T(128)}, s32[8]{0:T(128)}, s32[2]{0:T(128)}, s32[1,16,16]{2,1,0:T(8,128)}, ...), branch_computations={%region_0.1_spmd, %region_1.2_spmd} | conditional | flops 6989948928 | bytes 109653184 | solution.py:388
  1.5 4.1 %collective-permute-start.29 = (bf16[64,1536]{1,0:T(8,128)(2,1)}, bf16[64,1536]{1,0:T(8,128)(2,1)S(1)}, u32[]{:S(2)}, u32[]{:S(2)}) collective-permute-start(bf16[64,1536]{1,0:T(8,128)(2,1)} %get-tuple-element.75), channel_id=1, source_target_pairs={{0,4},{1,5},{2,6},{3,7},{4,0},{5,1},{6,2},{7,3},{8,12},{9,13},{10,... | collective-permute-start | bytes 589832 | tf_op jit(solution)/shard_map/cond/branch_1_fun/ppermute | solution.py:38
  6.6 2.4 %collective-permute-start.27 = (bf16[128,1024]{1,0:T(8,128)(2,1)S(1)}, bf16[128,1024]{1,0:T(8,128)(2,1)S(1)}, u32[]{:S(2)}, u32[]{:S(2)}) collective-permute-start(bf16[128,1024]{1,0:T(8,128)(2,1)S(1)} %bitcast.31), channel_id=1, source_target_pairs={{1,0},{2,1},{3,2},{4,3},{5,4},{6,5},{7,6},{0,7},{9,8},{10,9},{11,1... | collective-permute-start | bytes 786440 | tf_op jit(solution)/shard_map/cond/branch_1_fun/ppermute | solution.py:46
  10.3 5.5 %collective-permute-done.29 = bf16[64,1536]{1,0:T(8,128)(2,1)S(1)} collective-permute-done((bf16[64,1536]{1,0:T(8,128)(2,1)}, bf16[64,1536]{1,0:T(8,128)(2,1)S(1)}, u32[]{:S(2)}, u32[]{:S(2)}) %collective-permute-start.29) | collective-permute-done | bytes 196640 | tf_op jit(solution)/shard_map/cond/branch_1_fun/ppermute | solution.py:38
  16.8 3.2 %collective-permute-start.30 = (bf16[128,1536]{1,0:T(8,128)(2,1)S(1)}, bf16[128,1536]{1,0:T(8,128)(2,1)S(1)}, u32[]{:S(2)}, u32[]{:S(2)}) collective-permute-start(bf16[128,1536]{1,0:T(8,128)(2,1)S(1)} %pad_maximum_fusion.2), channel_id=1, source_target_pairs={{0,1},{1,0},{2,3},{3,2},{4,5},{5,4},{6,7},{7,6},{8,10},{9,11},{10,... | collective-permute-start | bytes 1179656 | tf_op jit(solution)/shard_map/cond/branch_1_fun/ppermute | solution.py:38
  20.9 4.8 %collective-permute-done.30 = bf16[128,1536]{1,0:T(8,128)(2,1)S(1)} collective-permute-done((bf16[128,1536]{1,0:T(8,128)(2,1)S(1)}, bf16[128,1536]{1,0:T(8,128)(2,1)S(1)}, u32[]{:S(2)}, u32[]{:S(2)}) %collective-permute-start.30) | collective-permute-done | bytes 393248 | tf_op jit(solution)/shard_map/cond/branch_1_fun/ppermute | solution.py:38
  25.8 4.5 %collective-permute-start.31 = (bf16[256,1536]{1,0:T(8,128)(2,1)S(1)}, bf16[256,1536]{1,0:T(8,128)(2,1)S(1)}, u32[]{:S(2)}, u32[]{:S(2)}) collective-permute-start(bf16[256,1536]{1,0:T(8,128)(2,1)S(1)} %constant_dynamic-update-slice_fusion.6.w0), channel_id=1, source_target_pairs={{0,2},{1,3},{2,0},{3,1},{4,6},{5,7},{6,4},{7,5},{8,9},{9,8},{10,11... | collective-permute-start | bytes 2359304 | tf_op jit(solution)/shard_map/cond/branch_1_fun/ppermute | solution.py:38
  31.1 1.3 %fusion.15 = s32[256]{0:T(256)S(1)} fusion(pred[]{:T(512)S(6)} %eq.45, s32[]{:T(128)} %bitcast.11, s32[]{:T(128)} %bitcast.10), kind=kLoop, calls=%fused_computation.93 | loop fusion | flops 4608 | bytes 1033 | tf_op jit(solution)/shard_map/cond/branch_1_fun/add | solution.py:295
  32.5 3.3 %collective-permute-start.36 = (bf16[32,1024]{1,0:T(8,128)(2,1)S(1)}, bf16[32,1024]{1,0:T(8,128)(2,1)S(1)}, u32[]{:S(2)}, u32[]{:S(2)}) collective-permute-start(bf16[32,1024]{1,0:T(8,128)(2,1)S(1)} %copy-done.5), channel_id=1, source_target_pairs={{0,4},{1,5},{2,6},{3,7},{4,0},{5,1},{6,2},{7,3},{8,12},{9,13},{10,... | collective-permute-start | bytes 196616 | tf_op jit(solution)/shard_map/cond/branch_1_fun/ppermute | solution.py:38
  35.8 5.9 %collective-permute-done.31.w1 = bf16[256,1536]{1,0:T(8,128)(2,1)S(1)} collective-permute-done((bf16[256,1536]{1,0:T(8,128)(2,1)S(1)}, bf16[256,1536]{1,0:T(8,128)(2,1)S(1)}, u32[]{:S(2)}, u32[]{:S(2)}) %collective-permute-start.31) | collective-permute-done | bytes 786464 | tf_op jit(solution)/shard_map/cond/branch_1_fun/ppermute | solution.py:38
  42.8 1.2 %norm.3 = (bf16[256,1024]{1,0:T(8,128)(2,1)S(1)}, bf16[256,1024]{1,0:T(8,128)(2,1)S(1)}, bf16[1024,256]{1,0:T(8,128)(2,1)S(1)}, f32[256,1]{1,0:T(8,128)S(1)}, f32[256,1]{1,0:T(8,128)S(1)}) custom-call(s32[2]{0:T(128)S(1)} %copy-done.7, s32[16]{0:T(128)S(1)} %pad_add_fusion.1.table.place_at.order, bf16[256,1024]{1,0:T(8,128)(2,1)S(1)} %bitcast.20, ...), custom_call_target="tpu_custom_call" | custom-call | flops 5242880 | bytes 2621440 | tf_op jit(solution)/shard_map/cond/branch_1_fun/norm/pallas_call | solution.py:304
  44.0 6.0 %collective-permute-start.35 = (bf16[128,1024]{1,0:T(8,128)(2,1)S(1)}, bf16[128,1024]{1,0:T(8,128)(2,1)S(1)}, u32[]{:S(2)}, u32[]{:S(2)}) collective-permute-start(bf16[128,1024]{1,0:T(8,128)(2,1)S(1)} %bitcast.28), channel_id=1, source_target_pairs={{1,0},{2,1},{3,2},{4,3},{5,4},{6,5},{7,6},{0,7},{9,8},{10,9},{11,1... | collective-permute-start | bytes 786440 | tf_op jit(solution)/shard_map/cond/branch_1_fun/ppermute | solution.py:46
  50.0 1.4 %collective-permute-start.38 = (bf16[128,1024]{1,0:T(8,128)(2,1)S(1)}, bf16[128,1024]{1,0:T(8,128)(2,1)S(1)}, u32[]{:S(2)}, u32[]{:S(2)}) collective-permute-start(bf16[128,1024]{1,0:T(8,128)(2,1)S(1)} %constant_dynamic-update-slice_fusion.9.w0), channel_id=1, source_target_pairs={{0,2},{1,3},{2,0},{3,1},{4,6},{5,7},{6,4},{7,5},{8,9},{9,8},{10,11... | collective-permute-start | bytes 786440 | tf_op jit(solution)/shard_map/cond/branch_1_fun/ppermute | solution.py:38
  51.4 3.3 %fwd.3 = (bf16[1024,1536]{1,0:T(8,128)(2,1)S(1)}, bf16[256,1536]{1,0:T(8,128)(2,1)S(1)}, f32[8,256,256]{2,1,0:T(8,128)S(1)}, bf16[256,512]{1,0:T(8,128)(2,1)S(1)}, bf16[512,256]{1,0:T(8,128)(2,1)S(1)}) custom-call(s32[16]{0:T(128)S(1)} %pad_add_fusion.1.table.place_at.order, s32[16]{0:T(128)S(1)} %pad_add_fusion.1.table.place_at.order, ...), custom_call_target="tpu_custom_call" | custom-call | flops 2415919104 | bytes 10485760 | tf_op jit(solution)/shard_map/cond/branch_1_fun/fwd/pallas_call | solution.py:313
  54.7 1.0 term_out.3
  57.1 1.0 collective-permute-done.39.w2
  58.6 3.3 %bwd_a.3 = (bf16[512,1024]{1,0:T(8,128)(2,1)S(1)}, bf16[256,512]{1,0:T(8,128)(2,1)S(1)}, bf16[256,768]{1,0:T(8,128)(2,1)S(1)}, f32[512,768]{1,0:T(8,128)S(1)}, bf16[512,768]{1,0:T(8,128)(2,1)S(1)}) custom-call(s32[16]{0:T(128)S(1)} %pad_add_fusion.1.table.place_at.order, bf16[256,1024]{1,0:T(8,128)(2,1)S(1)} %get-tuple-element.81.cot, ...), custom_call_target="tpu_custom_call" | custom-call | flops 1610612736 | bytes 6291456 | tf_op jit(solution)/shard_map/cond/branch_1_fun/bwd_a/pallas_call | solution.py:334
  62.4 2.5 %collective-permute-start.51 = (bf16[128,1024]{1,0:T(8,128)(2,1)S(1)}, bf16[128,1024]{1,0:T(8,128)(2,1)S(1)}, u32[]{:S(2)}, u32[]{:S(2)}) collective-permute-start(bf16[128,1024]{1,0:T(8,128)(2,1)S(1)} %slice.273), channel_id=1, source_target_pairs={{0,2},{1,3},{2,0},{3,1},{4,6},{5,7},{6,4},{7,5},{8,9},{9,8},{10,11... | collective-permute-start | bytes 786440 | tf_op jit(solution)/shard_map/cond/branch_1_fun/ppermute | solution.py:38
  66.3 2.2 %bwd_b.3 = (bf16[256,768]{1,0:T(8,128)(2,1)S(1)}, f32[512,768]{1,0:T(8,128)S(1)}, bf16[512,768]{1,0:T(8,128)(2,1)S(1)}) custom-call(bf16[256,1536]{1,0:T(8,128)(2,1)S(1)} %get-tuple-element.82.packed, f32[8,256,256]{2,1,0:T(8,128)S(1)} %get-tuple-element.83.attn, bf16[256,512]{1,0:T(8,128)(2,1)S(1)} %get-tuple-element.99.gctx, ...), custom_call_target="tpu_custom_call" | custom-call | flops 1610612736 | bytes 6291456 | tf_op jit(solution)/shard_map/cond/branch_1_fun/bwd_b/pallas_call | solution.py:343
  69.4 1.6 %collective-permute-start.52 = (bf16[64,1024]{1,0:T(8,128)(2,1)S(1)}, bf16[64,1024]{1,0:T(8,128)(2,1)S(1)}, u32[]{:S(2)}, u32[]{:S(2)}) collective-permute-start(bf16[64,1024]{1,0:T(8,128)(2,1)S(1)} %slice.276), channel_id=1, source_target_pairs={{0,1},{1,0},{2,3},{3,2},{4,5},{5,4},{6,7},{7,6},{8,10},{9,11},{10,... | collective-permute-start | bytes 393224 | tf_op jit(solution)/shard_map/cond/branch_1_fun/ppermute | solution.py:38
  71.2 2.5 %collective-permute-start.42 = (bf16[256,768]{1,0:T(8,128)(2,1)S(1)}, bf16[256,768]{1,0:T(8,128)(2,1)S(1)}, u32[]{:S(2)}, u32[]{:S(2)}) collective-permute-start(bf16[256,768]{1,0:T(8,128)(2,1)S(1)} %slice.272), channel_id=1, source_target_pairs={{0,2},{1,3},{2,0},{3,1},{4,6},{5,7},{6,4},{7,5},{8,9},{9,8},{10,11... | collective-permute-start | bytes 1179656 | tf_op jit(solution)/shard_map/cond/branch_1_fun/ppermute | solution.py:38
  74.6 1.3 %grad.3 = bf16[256,1024]{1,0:T(8,128)(2,1)S(1)} custom-call(bf16[256,1024]{1,0:T(8,128)(2,1)S(1)} %get-tuple-element.93.xw, f32[256,1]{1,0:T(8,128)S(1)} %get-tuple-element.94.mean, f32[256,1]{1,0:T(8,128)S(1)} %get-tuple-element.95.inv, bf16[256,768]{1,0:T(8,128)(2,1)S(1)} %get-tuple-element.96.gp_a, bf16[256,768]{1,0:T(8,128)(2,1)S(1)} %get-tuple-element.101.gp_b, ...), custom_call_target="tpu_custom_call" | custom-call | flops 805306368 | bytes 6291456 | tf_op jit(solution)/shard_map/cond/branch_1_fun/grad/pallas_call | solution.py:363
  77.1 1.1 %collective-permute-start.53 = (bf16[32,1024]{1,0:T(8,128)(2,1)S(1)}, bf16[32,1024]{1,0:T(8,128)(2,1)S(1)}, u32[]{:S(2)}, u32[]{:S(2)}) collective-permute-start(bf16[32,1024]{1,0:T(8,128)(2,1)S(1)} %slice.279), channel_id=1, source_target_pairs={{0,4},{1,5},{2,6},{3,7},{4,0},{5,1},{6,2},{7,3},{8,12},{9,13},{10,... | collective-permute-start | bytes 196616 | tf_op jit(solution)/shard_map/cond/branch_1_fun/ppermute | solution.py:38
  78.4 2.7 %collective-permute-start.48 = (bf16[256,768]{1,0:T(8,128)(2,1)S(1)}, bf16[256,768]{1,0:T(8,128)(2,1)S(1)}, u32[]{:S(2)}, u32[]{:S(2)}) collective-permute-start(bf16[256,768]{1,0:T(8,128)(2,1)S(1)} %slice.271), channel_id=1, source_target_pairs={{0,2},{1,3},{2,0},{3,1},{4,6},{5,7},{6,4},{7,5},{8,9},{9,8},{10,11... | collective-permute-start | bytes 1179656 | tf_op jit(solution)/shard_map/cond/branch_1_fun/ppermute | solution.py:38
  81.1 1.2 %collective-permute-done.53 = bf16[32,1024]{1,0:T(8,128)(2,1)S(1)} collective-permute-done((bf16[32,1024]{1,0:T(8,128)(2,1)S(1)}, bf16[32,1024]{1,0:T(8,128)(2,1)S(1)}, u32[]{:S(2)}, u32[]{:S(2)}) %collective-permute-start.53) | collective-permute-done | bytes 65568 | tf_op jit(solution)/shard_map/cond/branch_1_fun/ppermute | solution.py:38
  83.1 7.0 %collective-permute-start.45 = (bf16[128,768]{1,0:T(8,128)(2,1)S(1)}, bf16[128,768]{1,0:T(8,128)(2,1)S(1)}, u32[]{:S(2)}, u32[]{:S(2)}) collective-permute-start(bf16[128,768]{1,0:T(8,128)(2,1)S(1)} %slice.275), channel_id=1, source_target_pairs={{0,1},{1,0},{2,3},{3,2},{4,5},{5,4},{6,7},{7,6},{8,10},{9,11},{10,... | collective-permute-start | bytes 589832 | tf_op jit(solution)/shard_map/cond/branch_1_fun/ppermute | solution.py:38
  90.1 4.5 %collective-permute-start.49 = (bf16[128,768]{1,0:T(8,128)(2,1)S(1)}, bf16[128,768]{1,0:T(8,128)(2,1)S(1)}, u32[]{:S(2)}, u32[]{:S(2)}) collective-permute-start(bf16[128,768]{1,0:T(8,128)(2,1)S(1)} %slice.274), channel_id=1, source_target_pairs={{0,1},{1,0},{2,3},{3,2},{4,5},{5,4},{6,7},{7,6},{8,10},{9,11},{10,... | collective-permute-start | bytes 589832 | tf_op jit(solution)/shard_map/cond/branch_1_fun/ppermute | solution.py:38
  94.7 1.8 %collective-permute-start.46 = (bf16[64,768]{1,0:T(8,128)(2,1)S(1)}, bf16[64,768]{1,0:T(8,128)(2,1)S(1)}, u32[]{:S(2)}, u32[]{:S(2)}) collective-permute-start(bf16[64,768]{1,0:T(8,128)(2,1)S(1)} %slice.278), channel_id=1, source_target_pairs={{0,4},{1,5},{2,6},{3,7},{4,0},{5,1},{6,2},{7,3},{8,12},{9,13},{10,... | collective-permute-start | bytes 294920 | tf_op jit(solution)/shard_map/cond/branch_1_fun/ppermute | solution.py:38
  96.5 1.8 %collective-permute-done.49 = bf16[128,768]{1,0:T(8,128)(2,1)S(1)} collective-permute-done((bf16[128,768]{1,0:T(8,128)(2,1)S(1)}, bf16[128,768]{1,0:T(8,128)(2,1)S(1)}, u32[]{:S(2)}, u32[]{:S(2)}) %collective-permute-start.49) | collective-permute-done | bytes 196640 | tf_op jit(solution)/shard_map/cond/branch_1_fun/ppermute | solution.py:38
  98.4 1.8 %collective-permute-start.50 = (bf16[64,768]{1,0:T(8,128)(2,1)S(1)}, bf16[64,768]{1,0:T(8,128)(2,1)S(1)}, u32[]{:S(2)}, u32[]{:S(2)}) collective-permute-start(bf16[64,768]{1,0:T(8,128)(2,1)S(1)} %slice.277), channel_id=1, source_target_pairs={{0,4},{1,5},{2,6},{3,7},{4,0},{5,1},{6,2},{7,3},{8,12},{9,13},{10,... | collective-permute-start | bytes 294920 | tf_op jit(solution)/shard_map/cond/branch_1_fun/ppermute | solution.py:38
  101.1 1.8 %output.3 = bf16[256,1024]{1,0:T(8,128)(2,1)} custom-call(s32[2]{0:T(128)S(1)} %copy-done.7, bf16[256,1024]{1,0:T(8,128)(2,1)S(1)} %bitcast.21, bf16[256,512]{1,0:T(8,128)(2,1)S(1)} %get-tuple-element.77.ctx, bf16[128,512]{1,0:T(8,128)(2,1)S(1)} %collective-permute-done.34.back, bf16[512,1024]{1,0:T(8,128)(2,1)S(1)} %get-tuple-element.92.full), custom_call_target="tpu_custom_call" | custom-call | flops 268435456 | bytes 3145728 | tf_op jit(solution)/shard_map/cond/branch_1_fun/output/pallas_call | solution.py:373
  103.0 2.0 %collective-permute-done.50.last_b = bf16[64,768]{1,0:T(8,128)(2,1)S(1)} collective-permute-done((bf16[64,768]{1,0:T(8,128)(2,1)S(1)}, bf16[64,768]{1,0:T(8,128)(2,1)S(1)}, u32[]{:S(2)}, u32[]{:S(2)}) %collective-permute-start.50) | collective-permute-done | bytes 98336 | tf_op jit(solution)/shard_map/cond/branch_1_fun/ppermute | solution.py:38
  (89 shorter events, 15.7 us)
Async XLA Ops:
  1.5 28.9 %copy-start.3 = (bf16[1,16,16,1024]{3,2,1,0:T(8,128)(2,1)S(1)}, bf16[1,16,16,1024]{3,2,1,0:T(8,128)(2,1)}, u32[]{:S(2)}) copy-start(bf16[1,16,16,1024]{3,2,1,0:T(8,128)(2,1)} %get-tuple-element.79) | copy-start | bytes 1572868 | tf_op jit(solution)/shard_map/cond
  1.5 14.3 %collective-permute-start.29 = (bf16[64,1536]{1,0:T(8,128)(2,1)}, bf16[64,1536]{1,0:T(8,128)(2,1)S(1)}, u32[]{:S(2)}, u32[]{:S(2)}) collective-permute-start(bf16[64,1536]{1,0:T(8,128)(2,1)} %get-tuple-element.75), channel_id=1, source_target_pairs={{0,4},{1,5},{2,6},{3,7},{4,0},{5,1},{6,2},{7,3},{8,12},{9,13},{10,... | collective-permute-start | bytes 589832 | tf_op jit(solution)/shard_map/cond/branch_1_fun/ppermute | solution.py:38
  6.6 23.9 %copy-start.9 = (s32[8]{0:T(128)S(1)}, s32[8]{0:T(128)}, u32[]{:S(2)}) copy-start(s32[8]{0:T(128)} %get-tuple-element.71) | copy-start | bytes 100 | tf_op jit(solution)/shard_map/cond
  6.6 23.9 %copy-start.7 = (s32[2]{0:T(128)S(1)}, s32[2]{0:T(128)}, u32[]{:S(2)}) copy-start(s32[2]{0:T(128)} %get-tuple-element.69.scal) | copy-start | bytes 28 | tf_op jit(solution)/shard_map/cond
  6.6 25.8 %copy-start.5 = (bf16[32,1024]{1,0:T(8,128)(2,1)S(1)}, bf16[32,1024]{1,0:T(8,128)(2,1)}, u32[]{:S(2)}) copy-start(bf16[32,1024]{1,0:T(8,128)(2,1)} %get-tuple-element.86) | copy-start | bytes 196612 | tf_op jit(solution)/shard_map/cond
  6.6 10.2 %collective-permute-start.27 = (bf16[128,1024]{1,0:T(8,128)(2,1)S(1)}, bf16[128,1024]{1,0:T(8,128)(2,1)S(1)}, u32[]{:S(2)}, u32[]{:S(2)}) collective-permute-start(bf16[128,1024]{1,0:T(8,128)(2,1)S(1)} %bitcast.31), channel_id=1, source_target_pairs={{1,0},{2,1},{3,2},{4,3},{5,4},{6,5},{7,6},{0,7},{9,8},{10,9},{11,1... | collective-permute-start | bytes 786440 | tf_op jit(solution)/shard_map/cond/branch_1_fun/ppermute | solution.py:46
  9.8 7.0 %collective-permute-start.28 = (bf16[128,1]{0,1:T(2,128)(2,1)S(1)}, bf16[128,1]{0,1:T(2,128)(2,1)S(1)}, u32[]{:S(2)}, u32[]{:S(2)}) collective-permute-start(bf16[128,1]{0,1:T(2,128)(2,1)S(1)} %slice.165), channel_id=1, source_target_pairs={{1,0},{2,1},{3,2},{4,3},{5,4},{6,5},{7,6},{0,7},{9,8},{10,9},{11,1... | collective-permute-start | bytes 776 | tf_op jit(solution)/shard_map/cond/branch_1_fun/ppermute | solution.py:46
  16.8 26.1 %copy-start.1 = (bf16[1,16,16,1024]{3,2,1,0:T(8,128)(2,1)S(1)}, bf16[1,16,16,1024]{3,2,1,0:T(8,128)(2,1)}, u32[]{:S(2)}) copy-start(bf16[1,16,16,1024]{3,2,1,0:T(8,128)(2,1)} %get-tuple-element.70) | copy-start | bytes 1572868 | tf_op jit(solution)/shard_map/cond
  16.8 8.9 %collective-permute-start.30 = (bf16[128,1536]{1,0:T(8,128)(2,1)S(1)}, bf16[128,1536]{1,0:T(8,128)(2,1)S(1)}, u32[]{:S(2)}, u32[]{:S(2)}) collective-permute-start(bf16[128,1536]{1,0:T(8,128)(2,1)S(1)} %pad_maximum_fusion.2), channel_id=1, source_target_pairs={{0,1},{1,0},{2,3},{3,2},{4,5},{5,4},{6,7},{7,6},{8,10},{9,11},{10,... | collective-permute-start | bytes 1179656 | tf_op jit(solution)/shard_map/cond/branch_1_fun/ppermute | solution.py:38
  25.8 15.9 %collective-permute-start.31 = (bf16[256,1536]{1,0:T(8,128)(2,1)S(1)}, bf16[256,1536]{1,0:T(8,128)(2,1)S(1)}, u32[]{:S(2)}, u32[]{:S(2)}) collective-permute-start(bf16[256,1536]{1,0:T(8,128)(2,1)S(1)} %constant_dynamic-update-slice_fusion.6.w0), channel_id=1, source_target_pairs={{0,2},{1,3},{2,0},{3,1},{4,6},{5,7},{6,4},{7,5},{8,9},{9,8},{10,11... | collective-permute-start | bytes 2359304 | tf_op jit(solution)/shard_map/cond/branch_1_fun/ppermute | solution.py:38
  32.5 9.9 %collective-permute-start.36 = (bf16[32,1024]{1,0:T(8,128)(2,1)S(1)}, bf16[32,1024]{1,0:T(8,128)(2,1)S(1)}, u32[]{:S(2)}, u32[]{:S(2)}) collective-permute-start(bf16[32,1024]{1,0:T(8,128)(2,1)S(1)} %copy-done.5), channel_id=1, source_target_pairs={{0,4},{1,5},{2,6},{3,7},{4,0},{5,1},{6,2},{7,3},{8,12},{9,13},{10,... | collective-permute-start | bytes 196616 | tf_op jit(solution)/shard_map/cond/branch_1_fun/ppermute | solution.py:38
  35.8 15.6 %collective-permute-start.32 = (bf16[256,1536]{1,0:T(8,128)(2,1)S(1)}, bf16[256,1536]{1,0:T(8,128)(2,1)S(1)}, u32[]{:S(2)}, u32[]{:S(2)}) collective-permute-start(bf16[256,1536]{1,0:T(8,128)(2,1)S(1)} %constant_dynamic-update-slice_fusion.6.w0), channel_id=1, source_target_pairs={{0,8},{8,0},{1,9},{9,1},{2,10},{10,2},{3,11},{11,3},{4,12},{12,4},... | collective-permute-start | bytes 2359304 | tf_op jit(solution)/shard_map/cond/branch_1_fun/ppermute | solution.py:42
  41.7 9.7 %collective-permute-start.33 = (bf16[256,1536]{1,0:T(8,128)(2,1)S(1)}, bf16[256,1536]{1,0:T(8,128)(2,1)S(1)}, u32[]{:S(2)}, u32[]{:S(2)}) collective-permute-start(bf16[256,1536]{1,0:T(8,128)(2,1)S(1)} %collective-permute-done.31.w1), channel_id=1, source_target_pairs={{0,8},{8,0},{1,9},{9,1},{2,10},{10,2},{3,11},{11,3},{4,12},{12,4},... | collective-permute-start | bytes 2359304 | tf_op jit(solution)/shard_map/cond/branch_1_fun/ppermute | solution.py:42
  42.4 7.7 %collective-permute-start.37 = (bf16[64,1024]{1,0:T(8,128)(2,1)S(1)}, bf16[64,1024]{1,0:T(8,128)(2,1)S(1)}, u32[]{:S(2)}, u32[]{:S(2)}) collective-permute-start(bf16[64,1024]{1,0:T(8,128)(2,1)S(1)} %pad_maximum_fusion.3), channel_id=1, source_target_pairs={{0,1},{1,0},{2,3},{3,2},{4,5},{5,4},{6,7},{7,6},{8,10},{9,11},{10,... | collective-permute-start | bytes 393224 | tf_op jit(solution)/shard_map/cond/branch_1_fun/ppermute | solution.py:38
  44.0 10.7 %collective-permute-start.35 = (bf16[128,1024]{1,0:T(8,128)(2,1)S(1)}, bf16[128,1024]{1,0:T(8,128)(2,1)S(1)}, u32[]{:S(2)}, u32[]{:S(2)}) collective-permute-start(bf16[128,1024]{1,0:T(8,128)(2,1)S(1)} %bitcast.28), channel_id=1, source_target_pairs={{1,0},{2,1},{3,2},{4,3},{5,4},{6,5},{7,6},{0,7},{9,8},{10,9},{11,1... | collective-permute-start | bytes 786440 | tf_op jit(solution)/shard_map/cond/branch_1_fun/ppermute | solution.py:46
  50.0 7.0 %collective-permute-start.38 = (bf16[128,1024]{1,0:T(8,128)(2,1)S(1)}, bf16[128,1024]{1,0:T(8,128)(2,1)S(1)}, u32[]{:S(2)}, u32[]{:S(2)}) collective-permute-start(bf16[128,1024]{1,0:T(8,128)(2,1)S(1)} %constant_dynamic-update-slice_fusion.9.w0), channel_id=1, source_target_pairs={{0,2},{1,3},{2,0},{3,1},{4,6},{5,7},{6,4},{7,5},{8,9},{9,8},{10,11... | collective-permute-start | bytes 786440 | tf_op jit(solution)/shard_map/cond/branch_1_fun/ppermute | solution.py:38
  55.8 6.4 %collective-permute-start.43 = (bf16[256,1024]{1,0:T(8,128)(2,1)S(1)}, bf16[256,1024]{1,0:T(8,128)(2,1)S(1)}, u32[]{:S(2)}, u32[]{:S(2)}) collective-permute-start(bf16[256,1024]{1,0:T(8,128)(2,1)S(1)} %get-tuple-element.98), channel_id=1, source_target_pairs={{0,8},{8,0},{1,9},{9,1},{2,10},{10,2},{3,11},{11,3},{4,12},{12,4},... | collective-permute-start | bytes 1572872 | tf_op jit(solution)/shard_map/cond/branch_1_fun/ppermute | solution.py:42
  55.8 2.3 %collective-permute-start.39 = (bf16[128,1024]{1,0:T(8,128)(2,1)S(1)}, bf16[128,1024]{1,0:T(8,128)(2,1)S(1)}, u32[]{:S(2)}, u32[]{:S(2)}) collective-permute-start(bf16[128,1024]{1,0:T(8,128)(2,1)S(1)} %constant_dynamic-update-slice_fusion.9.w0), channel_id=1, source_target_pairs={{0,8},{8,0},{1,9},{9,1},{2,10},{10,2},{3,11},{11,3},{4,12},{12,4},... | collective-permute-start | bytes 786440 | tf_op jit(solution)/shard_map/cond/branch_1_fun/ppermute | solution.py:42
  57.1 1.5 %collective-permute-start.40 = (bf16[128,1024]{1,0:T(8,128)(2,1)S(1)}, bf16[128,1024]{1,0:T(8,128)(2,1)S(1)}, u32[]{:S(2)}, u32[]{:S(2)}) collective-permute-start(bf16[128,1024]{1,0:T(8,128)(2,1)S(1)} %collective-permute-done.38.w1), channel_id=1, source_target_pairs={{0,8},{8,0},{1,9},{9,1},{2,10},{10,2},{3,11},{11,3},{4,12},{12,4},... | collective-permute-start | bytes 786440 | tf_op jit(solution)/shard_map/cond/branch_1_fun/ppermute | solution.py:42
  61.9 9.1 %collective-permute-start.41 = (bf16[512,768]{1,0:T(8,128)(2,1)S(1)}, bf16[512,768]{1,0:T(8,128)(2,1)S(1)}, u32[]{:S(2)}, u32[]{:S(2)}) collective-permute-start(bf16[512,768]{1,0:T(8,128)(2,1)S(1)} %get-tuple-element.90), channel_id=1, source_target_pairs={{0,8},{8,0},{1,9},{9,1},{2,10},{10,2},{3,11},{11,3},{4,12},{12,4},... | collective-permute-start | bytes 2359304 | tf_op jit(solution)/shard_map/cond/branch_1_fun/ppermute | solution.py:42
  62.4 6.9 %collective-permute-start.51 = (bf16[128,1024]{1,0:T(8,128)(2,1)S(1)}, bf16[128,1024]{1,0:T(8,128)(2,1)S(1)}, u32[]{:S(2)}, u32[]{:S(2)}) collective-permute-start(bf16[128,1024]{1,0:T(8,128)(2,1)S(1)} %slice.273), channel_id=1, source_target_pairs={{0,2},{1,3},{2,0},{3,1},{4,6},{5,7},{6,4},{7,5},{8,9},{9,8},{10,11... | collective-permute-start | bytes 786440 | tf_op jit(solution)/shard_map/cond/branch_1_fun/ppermute | solution.py:38
  65.6 9.0 %collective-permute-start.34 = (bf16[128,512]{1,0:T(8,128)(2,1)S(1)}, bf16[128,512]{1,0:T(8,128)(2,1)S(1)}, u32[]{:S(2)}, u32[]{:S(2)}) collective-permute-start(bf16[128,512]{1,0:T(8,128)(2,1)S(1)} %slice.166), channel_id=1, source_target_pairs={{7,0},{0,1},{1,2},{2,3},{3,4},{4,5},{5,6},{6,7},{15,8},{8,9},{9,10... | collective-permute-start | bytes 393224 | tf_op jit(solution)/shard_map/cond/branch_1_fun/ppermute | solution.py:46
  68.5 9.7 %collective-permute-start.47 = (bf16[512,768]{1,0:T(8,128)(2,1)S(1)}, bf16[512,768]{1,0:T(8,128)(2,1)S(1)}, u32[]{:S(2)}, u32[]{:S(2)}) collective-permute-start(bf16[512,768]{1,0:T(8,128)(2,1)S(1)} %get-tuple-element.104), channel_id=1, source_target_pairs={{0,8},{8,0},{1,9},{9,1},{2,10},{10,2},{3,11},{11,3},{4,12},{12,4},... | collective-permute-start | bytes 2359304 | tf_op jit(solution)/shard_map/cond/branch_1_fun/ppermute | solution.py:42
  69.4 7.7 %collective-permute-start.52 = (bf16[64,1024]{1,0:T(8,128)(2,1)S(1)}, bf16[64,1024]{1,0:T(8,128)(2,1)S(1)}, u32[]{:S(2)}, u32[]{:S(2)}) collective-permute-start(bf16[64,1024]{1,0:T(8,128)(2,1)S(1)} %slice.276), channel_id=1, source_target_pairs={{0,1},{1,0},{2,3},{3,2},{4,5},{5,4},{6,7},{7,6},{8,10},{9,11},{10,... | collective-permute-start | bytes 393224 | tf_op jit(solution)/shard_map/cond/branch_1_fun/ppermute | solution.py:38
  71.2 11.8 %collective-permute-start.42 = (bf16[256,768]{1,0:T(8,128)(2,1)S(1)}, bf16[256,768]{1,0:T(8,128)(2,1)S(1)}, u32[]{:S(2)}, u32[]{:S(2)}) collective-permute-start(bf16[256,768]{1,0:T(8,128)(2,1)S(1)} %slice.272), channel_id=1, source_target_pairs={{0,2},{1,3},{2,0},{3,1},{4,6},{5,7},{6,4},{7,5},{8,9},{9,8},{10,11... | collective-permute-start | bytes 1179656 | tf_op jit(solution)/shard_map/cond/branch_1_fun/ppermute | solution.py:38
  75.9 24.2 %collective-permute-start.44 = (bf16[128,1024]{1,0:T(8,128)(2,1)S(1)}, bf16[128,1024]{1,0:T(8,128)(2,1)S(1)}, u32[]{:S(2)}, u32[]{:S(2)}) collective-permute-start(bf16[128,1024]{1,0:T(8,128)(2,1)S(1)} %slice.212), channel_id=1, source_target_pairs={{7,0},{0,1},{1,2},{2,3},{3,4},{4,5},{5,6},{6,7},{15,8},{8,9},{9,10... | collective-permute-start | bytes 786440 | tf_op jit(solution)/shard_map/cond/branch_1_fun/ppermute | solution.py:46
  77.1 5.2 %collective-permute-start.53 = (bf16[32,1024]{1,0:T(8,128)(2,1)S(1)}, bf16[32,1024]{1,0:T(8,128)(2,1)S(1)}, u32[]{:S(2)}, u32[]{:S(2)}) collective-permute-start(bf16[32,1024]{1,0:T(8,128)(2,1)S(1)} %slice.279), channel_id=1, source_target_pairs={{0,4},{1,5},{2,6},{3,7},{4,0},{5,1},{6,2},{7,3},{8,12},{9,13},{10,... | collective-permute-start | bytes 196616 | tf_op jit(solution)/shard_map/cond/branch_1_fun/ppermute | solution.py:38
  78.4 11.7 %collective-permute-start.48 = (bf16[256,768]{1,0:T(8,128)(2,1)S(1)}, bf16[256,768]{1,0:T(8,128)(2,1)S(1)}, u32[]{:S(2)}, u32[]{:S(2)}) collective-permute-start(bf16[256,768]{1,0:T(8,128)(2,1)S(1)} %slice.271), channel_id=1, source_target_pairs={{0,2},{1,3},{2,0},{3,1},{4,6},{5,7},{6,4},{7,5},{8,9},{9,8},{10,11... | collective-permute-start | bytes 1179656 | tf_op jit(solution)/shard_map/cond/branch_1_fun/ppermute | solution.py:38
  83.1 11.6 %collective-permute-start.45 = (bf16[128,768]{1,0:T(8,128)(2,1)S(1)}, bf16[128,768]{1,0:T(8,128)(2,1)S(1)}, u32[]{:S(2)}, u32[]{:S(2)}) collective-permute-start(bf16[128,768]{1,0:T(8,128)(2,1)S(1)} %slice.275), channel_id=1, source_target_pairs={{0,1},{1,0},{2,3},{3,2},{4,5},{5,4},{6,7},{7,6},{8,10},{9,11},{10,... | collective-permute-start | bytes 589832 | tf_op jit(solution)/shard_map/cond/branch_1_fun/ppermute | solution.py:38
  90.1 8.2 %collective-permute-start.49 = (bf16[128,768]{1,0:T(8,128)(2,1)S(1)}, bf16[128,768]{1,0:T(8,128)(2,1)S(1)}, u32[]{:S(2)}, u32[]{:S(2)}) collective-permute-start(bf16[128,768]{1,0:T(8,128)(2,1)S(1)} %slice.274), channel_id=1, source_target_pairs={{0,1},{1,0},{2,3},{3,2},{4,5},{5,4},{6,7},{7,6},{8,10},{9,11},{10,... | collective-permute-start | bytes 589832 | tf_op jit(solution)/shard_map/cond/branch_1_fun/ppermute | solution.py:38
  94.7 8.3 %collective-permute-start.46 = (bf16[64,768]{1,0:T(8,128)(2,1)S(1)}, bf16[64,768]{1,0:T(8,128)(2,1)S(1)}, u32[]{:S(2)}, u32[]{:S(2)}) collective-permute-start(bf16[64,768]{1,0:T(8,128)(2,1)S(1)} %slice.278), channel_id=1, source_target_pairs={{0,4},{1,5},{2,6},{3,7},{4,0},{5,1},{6,2},{7,3},{8,12},{9,13},{10,... | collective-permute-start | bytes 294920 | tf_op jit(solution)/shard_map/cond/branch_1_fun/ppermute | solution.py:38
  98.4 6.6 %collective-permute-start.50 = (bf16[64,768]{1,0:T(8,128)(2,1)S(1)}, bf16[64,768]{1,0:T(8,128)(2,1)S(1)}, u32[]{:S(2)}, u32[]{:S(2)}) collective-permute-start(bf16[64,768]{1,0:T(8,128)(2,1)S(1)} %slice.277), channel_id=1, source_target_pairs={{0,4},{1,5},{2,6},{3,7},{4,0},{5,1},{6,2},{7,3},{8,12},{9,13},{10,... | collective-permute-start | bytes 294920 | tf_op jit(solution)/shard_map/cond/branch_1_fun/ppermute | solution.py:38
  (1 other events, 23.9 us)
